TPU v7x, 256 devices: a whole 4x4x8 slice. The times are simulated.
256 devices in a mesh: cells: 16 (over z_hi, x, core), modes: 16 (over y, z_lo).
Axes of the slice: x: 4, y: 4, z: 8 (z_hi: 2, z_lo: 4; z = z_hi * 4 + z_lo), core: 2. Of those that a mesh axis runs over, the one named last changes fastest.
Arguments:
- hermite_coefficient_array: float32 [32, 64, 32, 2048], P('cells', None, None, 'modes'), may hold values from -6 to 6
- encounter_kernel_array: bfloat16 [14400, 120], replicated, may hold values from -0.046875 to 0.046875
- obstacle_indicator: int32 [32, 64, 32], P('cells'), may hold values 0 or 1
Outputs:
- moments_next: float32 [32, 64, 32, 2048], P('cells', None, None, 'modes')
All inputs are finite; a program needn't handle non-finite values. No bound on the sum of `obstacle_indicator` on one device may be relied on, other than what follows from the above.
Results may differ from a plain program's by a relative error of at most 0.0003.
Values sent between devices are 32-bit elements; how exact they have to be, the bound alone decides.
No kernel may reach another device: no remote copies, remote signals or barrier semaphores. Data moves between devices by JAX's collectives and lax.ppermute only.
A program may use at most 64 MiB of HBM per device.

v0:
```python
import math

import jax
import jax.numpy as jnp
from jax import lax
from jax.sharding import PartitionSpec as P

MA = 16
MB = 16
MC = 8
LDEG = 7
BASIS_SIZE = 120
MODES = 2048


CFL = 0.04
DTC = 0.2
PRECISE = lax.Precision.HIGHEST


def passed_along(shard, axis, by):
    length = lax.axis_size(axis)
    pairs = [(i, i + by) for i in range(length) if 0 <= i + by < length]
    return lax.ppermute(shard, axis, pairs)


def extended(cells, sides, width):
    for axis, dim in sides:
        count = lax.axis_size(axis)
        head = lax.slice_in_dim(cells, 0, width, axis=dim)
        tail = lax.slice_in_dim(cells, cells.shape[dim] - width, cells.shape[dim], axis=dim)
        cells = jnp.concatenate(
            [
                lax.ppermute(tail, axis, [(i, (i + 1) % count) for i in range(count)]),
                cells,
                lax.ppermute(head, axis, [((i + 1) % count, i) for i in range(count)]),
            ],
            axis=dim,
        )
    return cells


def digits(mode_index):
    digit_a = mode_index // (MB * MC)
    digit_b = mode_index // MC % MB
    digit_c = mode_index % MC
    return (digit_a, digit_b, digit_c)


def ladder(source, target, same_rest):
    level = target.astype(jnp.float32)
    down_term = jnp.where(same_rest & (source == target - 1), jnp.sqrt(level), 0.0)
    up_term = jnp.where(same_rest & (source == target + 1), jnp.sqrt(level + 1.0), 0.0)
    return down_term + up_term


def coupling(first_mode, local_modes):
    mode_index = first_mode + jnp.arange(local_modes, dtype=jnp.int32)
    source_a, source_b, source_c = digits(mode_index[:, None])
    target_a, target_b, target_c = digits(mode_index[None, :])
    same_a = source_a == target_a
    same_b = source_b == target_b
    same_c = source_c == target_c
    x_matrix = ladder(source_a, target_a, same_b & same_c)
    y_matrix = ladder(source_b, target_b, same_a & same_c)
    z_matrix = ladder(source_c, target_c, same_a & same_b)
    return (x_matrix, jnp.concatenate([y_matrix, z_matrix], 0))


def body(hermite_coefficient_array, encounter_kernel_array, obstacle_indicator):
    plane_count, rows_y, rows_z, local_modes = hermite_coefficient_array.shape
    block_size = MB * MC
    speed_x = 2.0 * math.sqrt(MA)
    speed_y = 2.0 * math.sqrt(MB)
    speed_z = 2.0 * math.sqrt(MC)
    all_index = jnp.arange(MODES, dtype=jnp.int32)
    all_a, all_b, all_c = digits(all_index)
    low_flags = (all_a + all_b + all_c <= LDEG).astype(jnp.int32)
    rank_all = jnp.cumsum(low_flags) - 1
    targets = jnp.arange(BASIS_SIZE, dtype=jnp.int32)
    first_mode = lax.axis_index("modes") * local_modes
    first_a = (first_mode // block_size).astype(jnp.float32)
    last_a = first_a + float(local_modes // block_size - 1)
    x_matrix, yz_matrix = coupling(first_mode, local_modes)
    full_matrix = jnp.concatenate([x_matrix, yz_matrix], 0)

    def across(first_axis_gradient):
        from_lower = passed_along(first_axis_gradient, "modes", 1)
        from_upper = passed_along(first_axis_gradient, "modes", -1)
        lower_term = jnp.sqrt(first_a) * from_lower
        upper_term = jnp.sqrt(last_a + 1.0) * from_upper
        return lower_term + upper_term

    def substep(center, behind, beyond, solid):
        first_axis_gradient = beyond - behind
        lap_x = beyond - 2.0 * center + behind
        next_y = jnp.roll(center, -1, 1)
        prev_y = jnp.roll(center, 1, 1)
        next_z = jnp.roll(center, -1, 2)
        prev_z = jnp.roll(center, 1, 2)
        diff_y = next_y - prev_y
        lap_y = next_y - 2.0 * center + prev_y
        diff_z = next_z - prev_z
        lap_z = next_z - 2.0 * center + prev_z
        flux = jnp.dot(
            jnp.concatenate([first_axis_gradient, diff_y, diff_z], -1),
            full_matrix,
            precision=PRECISE,
            preferred_element_type=jnp.float32,
        )
        flux = flux + across(first_axis_gradient)
        update = center + CFL * (
            -0.5 * flux + 0.5 * (speed_x * lap_x + speed_y * lap_y + speed_z * lap_z)
        )
        return jnp.where(solid[..., None] != 0, center, update)

    def widen(field):
        return extended(field, (("cells", 0),), 1)

    padded = widen(hermite_coefficient_array)
    middle = substep(hermite_coefficient_array, padded[:-2], padded[2:], obstacle_indicator)
    padded = widen(middle)
    transported = substep(middle, padded[:-2], padded[2:], obstacle_indicator)
    cell_count = plane_count * rows_y * rows_z
    rows = transported.reshape(cell_count, local_modes)
    local_flags = lax.dynamic_slice_in_dim(low_flags, first_mode, local_modes)
    local_rank = lax.dynamic_slice_in_dim(rank_all, first_mode, local_modes)
    selector = ((local_flags[:, None] == 1) & (local_rank[:, None] == targets[None, :])).astype(
        jnp.float32
    )
    share_rows = cell_count // lax.axis_size("modes")
    low = lax.psum_scatter(
        jnp.dot(rows, selector, precision=PRECISE, preferred_element_type=jnp.float32),
        "modes",
        scatter_dimension=0,
        tiled=True,
    )
    quadratic_factors = (
        (low[:, :, None] * low[:, None, :])
        .reshape(share_rows, BASIS_SIZE * BASIS_SIZE)
        .astype(jnp.bfloat16)
    )
    scattered_state = jnp.dot(
        quadratic_factors, encounter_kernel_array, preferred_element_type=jnp.float32
    )
    lifted = jnp.dot(
        lax.all_gather(scattered_state, "modes", axis=0, tiled=True),
        selector.T,
        precision=PRECISE,
        preferred_element_type=jnp.float32,
    )
    result = rows + DTC * lifted
    return result.reshape(plane_count, rows_y, rows_z, local_modes)


def solution(mesh):
    placed = (P("cells", None, None, "modes"), P(), P("cells", None, None))
    return jax.shard_map(
        body, mesh=mesh, in_specs=placed, out_specs=P("cells", None, None, "modes"), check_vma=False
    )
```

profile of v0, /device:TPU:6, one launch (start us, length us, event | category | flops | bytes accessed | tf_op | source)
XLA Modules:
  0.0 488.2 jit_solution(3035547686091999700)
XLA Ops:
  6.5 3.2 fusion.65
  9.7 1.7 collective-permute-start
  11.6 0.7 copy.7
  12.4 11.9 %collective-permute-done.1 = f32[1,64,32,128]{3,2,1,0:T(8,128)} collective-permute-done((f32[1,64,32,128]{3,2,1,0:T(8,128)}, f32[1,64,32,128]{3,2,1,0:T(8,128)}, u32[]{:S(2)}, u32[]{:S(2)}) %collective-permute-start.1) | collective-permute-done | bytes 1048608 | tf_op jit(solution)/shard_map/ppermute | solution.py:34
  24.3 2.7 fusion.23
  26.9 1.3 collective-permute-start.3
  28.2 4.7 collective-permute-start.2
  33.7 0.7 fusion.61
  34.4 1.1 fusion.16
  35.5 0.8 select_add_fusion.2
  36.3 35.2 %collective-permute-done.3 = f32[2,64,32,128]{3,2,1,0:T(8,128)S(1)} collective-permute-done((f32[2,64,32,128]{3,2,1,0:T(8,128)S(1)}, f32[2,64,32,128]{3,2,1,0:T(8,128)S(1)}, u32[]{:S(2)}, u32[]{:S(2)}) %collective-permute-start.3) | collective-permute-done | bytes 2097184 | tf_op jit(solution)/shard_map/ppermute | solution.py:24
  71.5 1.3 copy-done.8
  72.8 0.7 copy-done.9
  73.5 9.4 %add_select_fusion.1 = f32[2,64,32,128]{3,2,1,0:T(8,128)S(1)} fusion(f32[2,64,32,128]{3,2,1,0:T(8,128)S(1)} %copy-done.1, f32[2,64,32,128]{3,2,1,0:T(8,128)} %copy-done.8, f32[2,64,32,128]{3,2,1,0:T(8,128)} %copy-done.9, f32[2,63,32,128]{3,2,1,0:T(8,128)S(1)} %get-tuple-element.20, f32[2,1,32,128]{3,2,1,0:T(8,128)S(1)} %get-tuple-element.22, ...), kind=kOutput, calls=%fused_computation.16 | convolution fusion | flops 2433318912 | bytes 25366536 | tf_op jit(solution)/shard_map/dot_general | solution.py:105
  82.9 1.6 fusion.60
  84.9 59.8 %collective-permute-start.5 = (f32[1,64,32,128]{3,2,1,0:T(8,128)}, f32[1,64,32,128]{3,2,1,0:T(8,128)}, u32[]{:S(2)}, u32[]{:S(2)}) collective-permute-start(f32[1,64,32,128]{3,2,1,0:T(8,128)} %get-tuple-element.13), channel_id=1, source_target_pairs={{0,16},{16,32},{32,48},{48,64},{64,80},{80,96},{96,112},{112,128},... | collective-permute-start | bytes 3145736 | tf_op jit(solution)/shard_map/ppermute | solution.py:34
  145.7 0.8 slice_reduce_fusion
  147.3 10.0 %collective-permute-done.4 = f32[1,64,32,128]{3,2,1,0:T(8,128)} collective-permute-done((f32[1,64,32,128]{3,2,1,0:T(8,128)}, f32[1,64,32,128]{3,2,1,0:T(8,128)}, u32[]{:S(2)}, u32[]{:S(2)}) %collective-permute-start.4) | collective-permute-done | bytes 1048608 | tf_op jit(solution)/shard_map/ppermute | solution.py:36
  157.3 2.6 fusion.24
  160.0 1.3 collective-permute-start.7
  161.3 5.9 %collective-permute-start.6 = (f32[2,64,32,128]{3,2,1,0:T(8,128)S(1)}, f32[2,64,32,128]{3,2,1,0:T(8,128)}, u32[]{:S(2)}, u32[]{:S(2)}) collective-permute-start(f32[2,64,32,128]{3,2,1,0:T(8,128)S(1)} %fusion.24), channel_id=1, source_target_pairs={{0,1},{1,2},{2,3},{3,4},{4,5},{5,6},{6,7},{7,8},{8,9},{9,10},{10,1... | collective-permute-start | bytes 6291464 | tf_op jit(solution)/shard_map/ppermute | solution.py:24
  168.5 0.7 fusion.56
  169.7 52.6 %collective-permute-done.7 = f32[2,64,32,128]{3,2,1,0:T(8,128)S(1)} collective-permute-done((f32[2,64,32,128]{3,2,1,0:T(8,128)S(1)}, f32[2,64,32,128]{3,2,1,0:T(8,128)S(1)}, u32[]{:S(2)}, u32[]{:S(2)}) %collective-permute-start.7) | collective-permute-done | bytes 2097184 | tf_op jit(solution)/shard_map/ppermute | solution.py:24
  222.4 1.3 copy-done.10
  223.7 9.4 %add_select_fusion = f32[2,64,32,128]{3,2,1,0:T(8,128)S(1)} fusion(f32[2,64,32,128]{3,2,1,0:T(8,128)S(1)} %copy-done.3, f32[2,64,32,128]{3,2,1,0:T(8,128)} %copy-done.10, f32[2,64,32,128]{3,2,1,0:T(8,128)} %collective-permute-done.6, f32[2,63,32,128]{3,2,1,0:T(8,128)S(1)} %get-tuple-element.10, f32[2,1,32,128]{3,2,1,0:T(8,128)S(1)} %get-tuple-element.12, ...), kind=kOutput, calls=%fused_computation.15 | convolution fusion | flops 2433318912 | bytes 25366536 | tf_op jit(solution)/shard_map/dot_general | solution.py:105
  233.1 1.3 copy-done.4
  234.4 2.5 fusion.27
  237.0 149.5 %reduce-scatter.2.cloned.1.call-done = f32[256,120]{0,1:T(8,128)} async-done(((f32[4096,120]{0,1:T(8,128)}), f32[256,120]{0,1:T(8,128)}) %reduce-scatter.2.cloned.1.call-update) | async-done | bytes 122896 | tf_op jit(solution)/shard_map/reduce_scatter | solution.py:132
  386.5 3.7 multiply_convert_fusion
  390.3 2.8 fusion.66
  393.1 83.6 %all-gather.2.cloned.1.call-done = f32[4096,120]{1,0:T(8,128)} async-done(((f32[256,120]{1,0:T(8,128)}), f32[4096,120]{1,0:T(8,128)}) %all-gather.2.cloned.1.call-update) | async-done | bytes 1966096 | tf_op jit(solution)/shard_map/all_gather | solution.py:147
  476.6 4.7 fusion.12
  (57 shorter events, 5.0 us)
Async XLA Ops:
  6.5 383.7 %copy-start = (bf16[14400,120]{0,1:T(8,128)(2,1)S(1)}, bf16[14400,120]{0,1:T(8,128)(2,1)}, u32[]{:S(2)}) copy-start(bf16[14400,120]{0,1:T(8,128)(2,1)} %param.4) | copy-start | bytes 10368004
  6.5 5.0 %copy-start.5 = (s32[2,64,32]{1,2,0:T(8,128)S(1)}, s32[2,64,32]{1,2,0:T(8,128)}, u32[]{:S(2)}) copy-start(s32[2,64,32]{1,2,0:T(8,128)} %param.5) | copy-start | bytes 49156
  6.5 380.0 %reduce-scatter.2.cloned.1.call-start = ((), (), s32[]{:S(2)}) async-start(), calls=%async_computation.1 | async-start | bytes 2088960 | tf_op jit(solution)/shard_map/reduce_scatter | solution.py:132
  9.7 14.5 %collective-permute-start.1 = (f32[1,64,32,128]{3,2,1,0:T(8,128)}, f32[1,64,32,128]{3,2,1,0:T(8,128)}, u32[]{:S(2)}, u32[]{:S(2)}) collective-permute-start(f32[1,64,32,128]{3,2,1,0:T(8,128)} %get-tuple-element.23), channel_id=1, source_target_pairs={{0,16},{16,32},{32,48},{48,64},{64,80},{80,96},{96,112},{112,128},... | collective-permute-start | bytes 3145736 | tf_op jit(solution)/shard_map/ppermute | solution.py:34
  9.7 14.5 %collective-permute-start = (f32[1,64,32,128]{3,2,1,0:T(8,128)}, f32[1,64,32,128]{3,2,1,0:T(8,128)}, u32[]{:S(2)}, u32[]{:S(2)}) collective-permute-start(f32[1,64,32,128]{3,2,1,0:T(8,128)} %get-tuple-element.24), channel_id=1, source_target_pairs={{16,0},{32,16},{48,32},{64,48},{80,64},{96,80},{112,96},{128,112},... | collective-permute-start | bytes 3145736 | tf_op jit(solution)/shard_map/ppermute | solution.py:36
  12.4 20.6 %copy-start.1 = (f32[2,64,32,128]{3,2,1,0:T(8,128)S(1)}, f32[2,64,32,128]{3,2,1,0:T(8,128)}, u32[]{:S(2)}) copy-start(f32[2,64,32,128]{3,2,1,0:T(8,128)} %param.3) | copy-start | bytes 6291460
  26.9 44.5 %collective-permute-start.3 = (f32[2,64,32,128]{3,2,1,0:T(8,128)S(1)}, f32[2,64,32,128]{3,2,1,0:T(8,128)S(1)}, u32[]{:S(2)}, u32[]{:S(2)}) collective-permute-start(f32[2,64,32,128]{3,2,1,0:T(8,128)S(1)} %fusion.23), channel_id=1, source_target_pairs={{1,0},{2,1},{3,2},{4,3},{5,4},{6,5},{7,6},{8,7},{9,8},{10,9},{11,1... | collective-permute-start | bytes 6291464 | tf_op jit(solution)/shard_map/ppermute | solution.py:24
  28.2 43.2 %collective-permute-start.2 = (f32[2,64,32,128]{3,2,1,0:T(8,128)S(1)}, f32[2,64,32,128]{3,2,1,0:T(8,128)S(1)}, u32[]{:S(2)}, u32[]{:S(2)}) collective-permute-start(f32[2,64,32,128]{3,2,1,0:T(8,128)S(1)} %fusion.23), channel_id=1, source_target_pairs={{0,1},{1,2},{2,3},{3,4},{4,5},{5,6},{6,7},{7,8},{8,9},{9,10},{10,1... | collective-permute-start | bytes 6291464 | tf_op jit(solution)/shard_map/ppermute | solution.py:24
  34.4 39.1 %copy-start.6 = (pred[2,64,32]{2,1,0:T(8,128)(4,1)S(1)}, pred[2,64,32]{2,1,0:T(8,128)(4,1)}, u32[]{:S(2)}) copy-start(pred[2,64,32]{2,1,0:T(8,128)(4,1)} %copy.7) | copy-start | bytes 12292
  71.4 1.3 copy-start.8
  71.4 2.0 copy-start.9
  82.9 2.0 copy-start.2
  84.9 62.4 %collective-permute-start.5 = (f32[1,64,32,128]{3,2,1,0:T(8,128)}, f32[1,64,32,128]{3,2,1,0:T(8,128)}, u32[]{:S(2)}, u32[]{:S(2)}) collective-permute-start(f32[1,64,32,128]{3,2,1,0:T(8,128)} %get-tuple-element.13), channel_id=1, source_target_pairs={{0,16},{16,32},{32,48},{48,64},{64,80},{80,96},{96,112},{112,128},... | collective-permute-start | bytes 3145736 | tf_op jit(solution)/shard_map/ppermute | solution.py:34
  144.7 12.6 %collective-permute-start.4 = (f32[1,64,32,128]{3,2,1,0:T(8,128)}, f32[1,64,32,128]{3,2,1,0:T(8,128)}, u32[]{:S(2)}, u32[]{:S(2)}) collective-permute-start(f32[1,64,32,128]{3,2,1,0:T(8,128)} %get-tuple-element.14), channel_id=1, source_target_pairs={{16,0},{32,16},{48,32},{64,48},{80,64},{96,80},{112,96},{128,112},... | collective-permute-start | bytes 3145736 | tf_op jit(solution)/shard_map/ppermute | solution.py:36
  146.7 20.6 %copy-start.3 = (f32[2,64,32,128]{3,2,1,0:T(8,128)S(1)}, f32[2,64,32,128]{3,2,1,0:T(8,128)}, u32[]{:S(2)}) copy-start(f32[2,64,32,128]{3,2,1,0:T(8,128)} %copy-done.2) | copy-start | bytes 6291460
  160.0 62.4 %collective-permute-start.7 = (f32[2,64,32,128]{3,2,1,0:T(8,128)S(1)}, f32[2,64,32,128]{3,2,1,0:T(8,128)S(1)}, u32[]{:S(2)}, u32[]{:S(2)}) collective-permute-start(f32[2,64,32,128]{3,2,1,0:T(8,128)S(1)} %fusion.24), channel_id=1, source_target_pairs={{1,0},{2,1},{3,2},{4,3},{5,4},{6,5},{7,6},{8,7},{9,8},{10,9},{11,1... | collective-permute-start | bytes 6291464 | tf_op jit(solution)/shard_map/ppermute | solution.py:24
  161.3 62.4 %collective-permute-start.6 = (f32[2,64,32,128]{3,2,1,0:T(8,128)S(1)}, f32[2,64,32,128]{3,2,1,0:T(8,128)}, u32[]{:S(2)}, u32[]{:S(2)}) collective-permute-start(f32[2,64,32,128]{3,2,1,0:T(8,128)S(1)} %fusion.24), channel_id=1, source_target_pairs={{0,1},{1,2},{2,3},{3,4},{4,5},{5,6},{6,7},{7,8},{8,9},{9,10},{10,1... | collective-permute-start | bytes 6291464 | tf_op jit(solution)/shard_map/ppermute | solution.py:24
  169.2 54.5 %copy-start.7 = (pred[2,64,32]{2,1,0:T(8,128)(4,1)S(1)}, pred[2,64,32]{2,1,0:T(8,128)(4,1)}, u32[]{:S(2)}) copy-start(pred[2,64,32]{2,1,0:T(8,128)(4,1)} %copy.7) | copy-start | bytes 12292
  222.4 1.3 copy-start.10
  233.1 1.3 copy-start.4
  237.0 239.6 %all-gather.2.cloned.1.call-start = ((), (), s32[]{:S(2)}) async-start(), calls=%async_computation.2 | async-start | bytes 2228224 | tf_op jit(solution)/shard_map/all_gather | solution.py:147
Sparse Core Ops, SparseCore 0:
  237.1 149.3 reduce-scatter.1
  393.2 83.3 all-gather.1
where the time goes:
time: 488 us
  waiting for transfers between devices  343 us (70%)
  starting transfers between devices  74.7 us (15%)
  matrix products  28.8 us (6%)
  local copies, waits for them, and re-layouts  14.2 us (3%)
  between operations  13.8 us (3%)
  other arithmetic  13.3 us (3%)
    reduce_scatter x1, waiting for transfers between devices, body(): lax.psum_scatter(jnp.dot(rows, selector, precision=PRECISE, preferred_ele...  149 us
    ppermute x4, waiting for transfers between devices, passed_along(): return lax.ppermute(shard, axis, pairs)  87.8 us
    all_gather x1, waiting for transfers between devices, body(): lax.all_gather(scattered_state, 'modes', axis=0, tiled=True)  83.6 us
    ppermute x2, starting transfers between devices, extended(): lax.ppermute(tail, axis, [(i, (i + 1) % count) for i in range(count)])  59.8 us
    dot_general x2, matrix products, substep(): jnp.dot(jnp.concatenate([first_axis_gradient, diff_y, diff_z], -1), full_...  18.8 us
    ppermute x4, starting transfers between devices, passed_along(): return lax.ppermute(shard, axis, pairs)  13.2 us
    ppermute x2, waiting for transfers between devices, extended(): lax.ppermute(tail, axis, [(i, (i + 1) % count) for i in range(count)])  12.5 us
    ppermute x2, waiting for transfers between devices, extended(): lax.ppermute(head, axis, [((i + 1) % count, i) for i in range(count)])  10 us
  transfers between devices with their start and end apart: 10, of which 7 were waited for; matrix products, arithmetic and copies ran while one was open for 2% of the time, Pallas kernels for 0%

commit v1 on v0

v1 whole, which is shorter than its diff:
```python
import functools
import math

import jax
import jax.numpy as jnp
import numpy as np
from jax import lax
from jax.experimental import pallas as pl
from jax.experimental.pallas import tpu as pltpu
from jax.sharding import Mesh, PartitionSpec as P

MA = 16
MB = 16
MC = 8
LDEG = 7
BASIS_SIZE = 120
LANES = MB * MC
LOW_A = LDEG + 1
PAD = 128
CFL = 0.04
DTC = 0.2
HALF = 0.5 * CFL
CX = HALF * 2.0 * math.sqrt(MA)
CY = HALF * 2.0 * math.sqrt(MB)
CZ = HALF * 2.0 * math.sqrt(MC)
CENTER = 2.0 * (CX + CY + CZ)
ROWS = 8
COLS = 8
GROUP = 8

AXES = ("half", "column", "core", "row", "run")
SIZES = (2, 4, 2, 4, 4)


def pairs(move):
    out = []
    for source in np.ndindex(*SIZES):
        target = move(*source)
        out.append((int(np.ravel_multi_index(source, SIZES)), int(np.ravel_multi_index(target, SIZES))))
    return out


def along_x(by):
    def move(half, column, core, row, run):
        place = (column * 2 + core + by) % 8
        return (half, place // 2, place % 2, row, run)

    return pairs(move)


def along_y(by):
    def move(half, column, core, row, run):
        place = (half * 4 + run + by) % 8
        return (place // 4, column, core, row, place % 4)

    return pairs(move)


def along_z(by):
    return pairs(lambda half, column, core, row, run: (half, column, core, (row + by) % 4, run))


def other_half():
    return pairs(lambda half, column, core, row, run: (1 - half, column, core, row, run))


def send(value, route):
    return lax.ppermute(value, AXES, route)


def ladder_rows():
    lane = lax.broadcasted_iota(jnp.int32, (COLS, LANES), 1)
    b = lane // MC
    c = lane % MC
    b_low = HALF * jnp.sqrt(b.astype(jnp.float32))
    b_high = jnp.where(b < MB - 1, HALF * jnp.sqrt((b + 1).astype(jnp.float32)), 0.0)
    c_low = HALF * jnp.sqrt(c.astype(jnp.float32))
    c_high = jnp.where(c < MC - 1, HALF * jnp.sqrt((c + 1).astype(jnp.float32)), 0.0)
    return b_low, b_high, c_low, c_high


def advance(flags, first, second, x_back, x_next, y_back, y_next, z_back, z_next, open_cells, put):
    b_low, b_high, c_low, c_high = ladder_rows()
    depth = lax.broadcasted_iota(jnp.int32, (COLS, LANES), 0)
    at_start = depth == 0
    at_end = depth == COLS - 1

    def block(g, carry):
        g_back = jnp.where(flags[0] != 0, 1 - g, g)
        g_next = jnp.where(flags[1] != 0, 1 - g, g)
        for p in range(2):
            here = (first, second)[p]
            for y in range(ROWS):

                def sides(a):
                    if p == 0:
                        back = x_back[g_back, a, y]
                        ahead = second[g, a, y]
                    else:
                        back = first[g, a, y]
                        ahead = x_next[g_next, a, y]
                    return ahead - back, ahead + back

                is_open = open_cells[g, p, y]
                before = None
                now = sides(0)
                for a in range(MA):
                    after = sides(a + 1) if a + 1 < MA else None
                    f = here[g, a, y]
                    yb = here[g, a, y - 1] if y > 0 else y_back[g, a, p]
                    yn = here[g, a, y + 1] if y + 1 < ROWS else y_next[g, a, p]
                    zb = jnp.where(at_start, z_back[g, a, p, y : y + 1, :], pltpu.roll(f, 1, 0))
                    zn = jnp.where(at_end, z_next[g, a, p, y : y + 1, :], pltpu.roll(f, COLS - 1, 0))
                    dy = yn - yb
                    dz = zn - zb
                    change = CX * now[1] + CY * (yn + yb) + CZ * (zn + zb) - CENTER * f
                    if before is not None:
                        change = change - (HALF * math.sqrt(a)) * before
                    if after is not None:
                        change = change - (HALF * math.sqrt(a + 1)) * after[0]
                    change = change - b_low * pltpu.roll(dy, MC, 1)
                    change = change - b_high * pltpu.roll(dy, LANES - MC, 1)
                    change = change - c_low * pltpu.roll(dz, 1, 1)
                    change = change - c_high * pltpu.roll(dz, LANES - 1, 1)
                    put(g, a, p, y, f + is_open * change)
                    before = now[0]
                    now = after
        return carry

    lax.fori_loop(0, 2, block, 0)


def first_kernel(
    flags, first, second, x_back, x_next, y_back, y_next, z_back, z_next, open_cells,
    out_first, out_second, out_y0, out_y7, out_z0, out_z7,
):
    def put(g, a, p, y, value):
        (out_first, out_second)[p][g, a, y] = value
        if y == 0:
            out_y0[g, a, p] = value
        if y == ROWS - 1:
            out_y7[g, a, p] = value
        out_z0[g, a, p, y : y + 1, :] = value[0:1]
        out_z7[g, a, p, y : y + 1, :] = value[COLS - 1 : COLS]

    advance(flags, first, second, x_back, x_next, y_back, y_next, z_back, z_next, open_cells, put)


def three_parts(value):
    high = value.astype(jnp.bfloat16)
    rest = value - high.astype(jnp.float32)
    middle = rest.astype(jnp.bfloat16)
    low = (rest - middle.astype(jnp.float32)).astype(jnp.bfloat16)
    return high, middle, low


def second_kernel(
    flags, first, second, x_back, x_next, y_back, y_next, z_back, z_next, open_cells,
    selector, weights, out, low, factors,
):
    def put(g, a, p, y, value):
        out[g, a, p, y] = value

    advance(flags, first, second, x_back, x_next, y_back, y_next, z_back, z_next, open_cells, put)
    cells = 2 * 2 * ROWS * COLS

    def plane(a):
        parts = [out[g, a, p].reshape(ROWS * COLS, LANES) for g in range(2) for p in range(2)]
        return jnp.concatenate(parts, 0)

    picked = jnp.zeros((PAD, cells), jnp.float32)
    for a in range(LOW_A):
        for part in three_parts(plane(a)):
            picked = picked + lax.dot_general(
                selector[a], part, (((1,), (1,)), ((), ())), preferred_element_type=jnp.float32
            )
    low[...] = picked

    def collide(step, total):
        base = step * GROUP
        for i in range(GROUP):
            row = low[pl.ds(base + i, 1), :]
            factors[i * PAD : (i + 1) * PAD, :] = (low[...] * row).astype(jnp.bfloat16)
        columns = pl.ds(pl.multiple_of(base * PAD, GROUP * PAD), GROUP * PAD)
        return total + jnp.dot(weights[:, columns], factors[...], preferred_element_type=jnp.float32)

    rate = lax.fori_loop(0, BASIS_SIZE // GROUP, collide, jnp.zeros((PAD, cells), jnp.float32))
    rate_parts = three_parts(jnp.transpose(DTC * rate))
    for a in range(LOW_A):
        lifted = jnp.zeros((cells, LANES), jnp.float32)
        for part in rate_parts:
            lifted = lifted + jnp.dot(part, selector[a], preferred_element_type=jnp.float32)
        for g in range(2):
            for p in range(2):
                at = (g * 2 + p) * ROWS * COLS
                block = lifted[at : at + ROWS * COLS].reshape(ROWS, COLS, LANES)
                out[g, a, p] = out[g, a, p] + block


def low_selector():
    rank = 0
    table = np.zeros((LOW_A, PAD, LANES), np.float32)
    for a in range(MA):
        for b in range(MB):
            for c in range(MC):
                if a + b + c <= LDEG:
                    table[a, rank, b * MC + c] = 1.0
                    rank += 1
    return jnp.asarray(table, jnp.bfloat16)


VMEM = pl.BlockSpec(memory_space=pltpu.VMEM)
SMEM = pl.BlockSpec(memory_space=pltpu.SMEM)
PARAMS = pltpu.CompilerParams(vmem_limit_bytes=48 << 20)


def f32(*shape):
    return jax.ShapeDtypeStruct(shape, jnp.float32)


def halos(first, second, y0, y7, z0, z7):
    x_back = send(second, along_x(1))
    x_next = send(first, along_x(-1))
    y_back = send(y7, along_y(1))
    y_next = send(y0, along_y(-1))
    z_back = send(z7, along_z(1))
    z_next = send(z0, along_z(-1))
    return x_back, x_next, y_back, y_next, z_back, z_next


def body(field, kernel_table, obstacles):
    half = lax.axis_index("half")
    place = lax.axis_index("column") * 2 + lax.axis_index("core")
    flags = jnp.stack([place == 0, place == 7]).astype(jnp.int32)

    run = lax.axis_index("run")
    row = lax.axis_index("row")
    tiles = obstacles.reshape(2, 2, 4, ROWS, 4, COLS)
    tiles = lax.dynamic_index_in_dim(tiles, run, 2, keepdims=False)
    tiles = lax.dynamic_index_in_dim(tiles, row, 3, keepdims=False)
    gas = (tiles == 0).astype(jnp.float32)
    mine = lax.dynamic_index_in_dim(gas, half, 1, keepdims=False)
    for_other = lax.dynamic_index_in_dim(gas, 1 - half, 1, keepdims=False)
    theirs = send(for_other, other_half())
    both = jnp.where(half == 0, jnp.stack([mine, theirs]), jnp.stack([theirs, mine]))
    open_cells = jnp.broadcast_to(both[..., None], (2, 2, ROWS, COLS, LANES))

    blocks = field.reshape(2, 2, 4, ROWS, 4, COLS, LANES).transpose(1, 4, 2, 0, 3, 5, 6)
    blocks = blocks.reshape(32, 2, ROWS, COLS, LANES)
    state = lax.all_to_all(blocks, ("half", "row", "run"), 0, 0, tiled=True)
    state = state.reshape(2, MA, 2, ROWS, COLS, LANES)

    first = state[:, :, 0]
    second = state[:, :, 1]
    edges = (state[:, :, :, 0], state[:, :, :, ROWS - 1], state[..., 0, :], state[..., COLS - 1, :])
    around = halos(first, second, *edges)
    plane = f32(2, MA, ROWS, COLS, LANES)
    edge = f32(2, MA, 2, ROWS, LANES)
    first, second, *edges = pl.pallas_call(
        first_kernel,
        out_shape=(plane, plane, edge, edge, edge, edge),
        in_specs=[SMEM] + [VMEM] * 9,
        out_specs=(VMEM,) * 6,
        compiler_params=PARAMS,
    )(flags, first, second, *around, open_cells)

    around = halos(first, second, *edges)
    weights = kernel_table.reshape(BASIS_SIZE, BASIS_SIZE, BASIS_SIZE).transpose(2, 0, 1)
    weights = jnp.pad(weights, ((0, PAD - BASIS_SIZE), (0, 0), (0, PAD - BASIS_SIZE)))
    weights = weights.reshape(PAD, BASIS_SIZE * PAD)
    cells = 2 * 2 * ROWS * COLS
    state = pl.pallas_call(
        second_kernel,
        out_shape=f32(2, MA, 2, ROWS, COLS, LANES),
        in_specs=[SMEM] + [VMEM] * 11,
        out_specs=VMEM,
        scratch_shapes=[pltpu.VMEM((PAD, cells), jnp.float32), pltpu.VMEM((GROUP * PAD, cells), jnp.bfloat16)],
        compiler_params=PARAMS,
    )(flags, first, second, *around, open_cells, low_selector(), weights)

    back = lax.all_to_all(
        state.reshape(32, 2, ROWS, COLS, LANES), ("half", "row", "run"), 0, 0, tiled=True
    )
    back = back.reshape(2, 4, 4, 2, ROWS, COLS, LANES).transpose(3, 0, 2, 4, 1, 5, 6)
    return back.reshape(2, 64, 32, LANES)


def solution(mesh):
    named = Mesh(mesh.devices.reshape(SIZES), AXES)
    cells = ("half", "column", "core")
    modes = ("row", "run")
    placed = (P(cells, None, None, modes), P(), P(cells, None, None))
    return jax.shard_map(
        body, mesh=named, in_specs=placed, out_specs=P(cells, None, None, modes), check_vma=False
    )
```

time: 488 us -> 196 us (0.40)
  waiting for transfers between devices: 343 us -> 8.83 us
  blocking collectives: 0 us -> 119 us
  starting transfers between devices: 74.7 us -> 16.6 us
  matrix products: 28.8 us -> 0 us
  local copies, waits for them, and re-layouts: 14.2 us -> 31.6 us
  Pallas kernels: 0 us -> 17 us
  between operations: 13.8 us -> 0.14 us
  other arithmetic: 13.3 us -> 0.11 us
    reduce_scatter x1 -> x0, waiting for transfers between devices: 149 us -> none  [body(): lax.psum_scatter(jnp.dot(rows, selector, precision=PRECISE, preferred_ele...]
    all_to_all x0 -> x2, blocking collectives: none -> 119 us  [the longest x1 62.4 us: body(): state = lax.all_to_all(blocks, ('half', 'row', 'run'), 0, 0, tiled=True)]
    ppermute x8 -> x13, waiting for transfers between devices: 110 us -> 8.83 us  [send(): return lax.ppermute(value, AXES, route)]
    all_gather x1 -> x0, waiting for transfers between devices: 83.6 us -> none  [body(): lax.all_gather(scattered_state, 'modes', axis=0, tiled=True)]
    ppermute x8 -> x13, starting transfers between devices: 74.7 us -> 16.6 us  [send(): return lax.ppermute(value, AXES, route)]
    dot_general x5 -> x0, matrix products: 28.8 us -> none  [the longest x2 18.8 us: substep(): jnp.dot(jnp.concatenate([first_axis_gradient, diff_y, diff_z], -1), full_...]
    pallas_call x0 -> x2, Pallas kernels: none -> 17 us  [the longest x1 11.4 us: body(): pl.pallas_call(second_kernel, out_shape=f32(2, MA, 2, ROWS, COLS, LANES),...]
    reshape x0 -> x4, local copies, waits for them, and re-layouts: none -> 12.3 us  [the longest x1 7.7 us: body(): kernel_table.reshape(BASIS_SIZE, BASIS_SIZE, BASIS_SIZE).transpose(2, 0, 1)]
  transfers between devices with their start and end apart: 10 -> 13, of which waited for: 7 -> 2; matrix products, arithmetic and copies ran while one was open for 2% -> 13% of each run, Pallas kernels for 0% -> 0%
where the time goes in v1:
time: 196 us; the launch traced here: 194 us
  blocking collectives  119 us (61%)
  local copies, waits for them, and re-layouts  31.6 us (16%)
  Pallas kernels  17 us (9%)
  starting transfers between devices  16.6 us (8%)
  waiting for transfers between devices  8.83 us (5%)
    all_to_all x1, blocking collectives, body(): state = lax.all_to_all(blocks, ('half', 'row', 'run'), 0, 0, tiled=True)  62.4 us
    all_to_all x1, blocking collectives, body(): lax.all_to_all(state.reshape(32, 2, ROWS, COLS, LANES), ('half', 'row', '...  56.9 us
    ppermute x13, starting transfers between devices, send(): return lax.ppermute(value, AXES, route)  16.6 us
    pallas_call x1, Pallas kernels, body(): pl.pallas_call(second_kernel, out_shape=f32(2, MA, 2, ROWS, COLS, LANES),...  11.4 us
    ppermute x13, waiting for transfers between devices, send(): return lax.ppermute(value, AXES, route)  8.83 us
    reshape x1, local copies, waits for them, and re-layouts, body(): kernel_table.reshape(BASIS_SIZE, BASIS_SIZE, BASIS_SIZE).transpose(2, 0, 1)  7.7 us
    ppermute x4, local copies, waits for them, and re-layouts, send(): return lax.ppermute(value, AXES, route)  5.93 us
    pallas_call x1, Pallas kernels, body(): pl.pallas_call(first_kernel, out_shape=(plane, plane, edge, edge, edge, e...  5.59 us
  transfers between devices with their start and end apart: 13, of which 2 were waited for; matrix products, arithmetic and copies ran while one was open for 13% of the time, Pallas kernels for 0%

profile of v1, /device:TPU:6, one launch (start us, length us, event | category | flops | bytes accessed | tf_op | source)
XLA Modules:
  0.0 193.6 jit_solution(1014252745001194571)
XLA Ops:
  0.0 2.8 %copy.23 = f32[2,2,4,8,4,8,128]{6,3,0,5,2,4,1:T(8,128)S(1)} copy(f32[2,2,4,8,4,8,128]{6,5,4,3,2,1,0:T(8,128)} %bitcast.43) | data formatting | bytes 4194304 | tf_op jit(solution)/shard_map/reshape | solution.py:248
  2.8 62.4 %all_to_all.10 = f32[32,2,8,8,128]{4,2,1,3,0:T(8,128)S(1)} all-to-all(f32[32,2,8,8,128]{4,2,1,3,0:T(8,128)S(1)} %bitcast.41), channel_id=1, replica_groups=mesh['half'=2,'column'=4,'core'=2,'row'=4,'run'=4] {'half','row','run'}, dimensions={0} | all-to-all | bytes 4194304 | tf_op jit(solution)/shard_map/all_to_all | solution.py:250
  65.2 0.2 copy.24
  65.4 1.6 slice_bitcast_fusion
  67.0 1.7 collective-permute-start.1
  68.8 0.2 reshape.73
  69.0 0.5 fusion
  69.5 0.4 collective-permute-start.2
  70.0 3.2 %collective-permute-start.6 = (f32[2,8,8]{2,1,0:T(8,128)S(1)}, f32[2,8,8]{2,1,0:T(8,128)S(1)}, u32[]{:S(2)}, u32[]{:S(2)}) collective-permute-start(f32[2,8,8]{2,1,0:T(8,128)S(1)} %bitcast.47), channel_id=1, source_target_pairs={{0,128},{1,129},{2,130},{3,131},{4,132},{5,133},{6,134},{7,135},{8... | collective-permute-start | bytes 1544 | tf_op jit(solution)/shard_map/ppermute | solution.py:68
  73.2 0.9 collective-permute-start.3
  74.2 0.8 slice_bitcast_fusion.2
  75.0 3.5 %collective-permute-done.6 = f32[2,8,8]{2,1,0:T(8,128)S(1)} collective-permute-done((f32[2,8,8]{2,1,0:T(8,128)S(1)}, f32[2,8,8]{2,1,0:T(8,128)S(1)}, u32[]{:S(2)}, u32[]{:S(2)}) %collective-permute-start.6) | collective-permute-done | bytes 544 | tf_op jit(solution)/shard_map/ppermute | solution.py:68
  78.5 1.8 collective-permute-start.5
  80.3 0.2 collective-permute-start.4
  80.7 2.8 %copy.28.second = f32[2,16,8,8,128]{4,3,2,1,0:T(8,128)} copy(f32[2,16,8,8,128]{4,2,1,0,3:T(8,128)} %get-tuple-element.21) | data formatting | bytes 2097152 | tf_op jit(solution)/shard_map/squeeze | solution.py:254
  83.5 1.8 copy.27.first
  85.3 0.2 copy.31.y_back
  85.5 0.2 copy.32.y_next
  85.7 2.8 %copy.29.x_back = f32[2,16,8,8,128]{4,3,2,1,0:T(8,128)} copy(f32[2,16,8,8,128]{4,2,1,0,3:T(8,128)} %collective-permute-done) | data formatting | bytes 2097152 | tf_op jit(solution)/shard_map/ppermute | solution.py:68
  88.5 2.8 %copy.30.x_next = f32[2,16,8,8,128]{4,3,2,1,0:T(8,128)} copy(f32[2,16,8,8,128]{4,2,1,0,3:T(8,128)} %collective-permute-done.1) | data formatting | bytes 2097152 | tf_op jit(solution)/shard_map/ppermute | solution.py:68
  91.4 5.6 %shard_map.46 = (f32[2,16,8,8,128]{4,3,2,1,0:T(8,128)S(1)}, f32[2,16,8,8,128]{4,3,2,1,0:T(8,128)S(1)}, f32[2,16,2,8,128]{4,3,2,1,0:T(8,128)}, f32[2,16,2,8,128]{...) custom-call(s32[2]{0:T(128)S(1)} %add_convert_fusion.flags, ...), custom_call_target="tpu_custom_call" | custom-call | tf_op jit(solution)/shard_map/pallas_call | solution.py:259
  97.0 0.5 collective-permute-start.7
  97.6 3.2 %collective-permute-start.10 = (f32[2,16,2,8,128]{4,3,2,1,0:T(8,128)}, f32[2,16,2,8,128]{4,3,2,1,0:T(8,128)}, u32[]{:S(2)}, u32[]{:S(2)}) collective-permute-start(f32[2,16,2,8,128]{4,3,2,1,0:T(8,128)} %get-tuple-element.14), channel_id=1, source_target_pairs={{0,131},{1,0},{2,1},{3,2},{4,135},{5,4},{6,5},{7,6},{8,139},{9,8},... | collective-permute-start | bytes 786440 | tf_op jit(solution)/shard_map/ppermute | solution.py:68
  100.8 1.7 collective-permute-start.11
  102.5 5.3 %collective-permute-done.9.y_back = f32[2,16,2,8,128]{4,3,2,1,0:T(8,128)S(1)} collective-permute-done((f32[2,16,2,8,128]{4,3,2,1,0:T(8,128)S(1)}, f32[2,16,2,8,128]{4,3,2,1,0:T(8,128)S(1)}, u32[]{:S(2)}, u32[]{:S(2)}) %collective-permute-start.9) | collective-permute-done | bytes 262176 | tf_op jit(solution)/shard_map/ppermute | solution.py:68
  107.8 2.8 %collective-permute-start.12 = (f32[2,16,2,8,128]{4,3,2,1,0:T(8,128)}, f32[2,16,2,8,128]{4,3,2,1,0:T(8,128)}, u32[]{:S(2)}, u32[]{:S(2)}) collective-permute-start(f32[2,16,2,8,128]{4,3,2,1,0:T(8,128)} %get-tuple-element.16), channel_id=1, source_target_pairs={{0,12},{1,13},{2,14},{3,15},{4,0},{5,1},{6,2},{7,3},{8,4},{9,5},{1... | collective-permute-start | bytes 786440 | tf_op jit(solution)/shard_map/ppermute | solution.py:68
  110.6 7.7 %reshape.74 = bf16[120,120,120]{1,0,2:T(8,128)(2,1)} reshape(bf16[14400,120]{0,1:T(8,128)(2,1)} %param.5) | data formatting | bytes 6912000 | tf_op jit(solution)/shard_map/reshape | solution.py:268
  118.3 2.8 %pad.4 = bf16[128,120,128]{2,1,0:T(8,128)(2,1)S(1)} pad(bf16[120,120,120]{2,1,0:T(8,128)(2,1)} %bitcast.36, bf16[]{:T(256)} %constant.80.clone.1), padding=0_8x0_0x0_8 | pad | bytes 7388162 | tf_op jit(solution)/shard_map/jit(_pad)/pad | solution.py:269
  121.1 2.6 %copy.36 = bf16[16,8,120,128]{3,1,2,0:T(8,128)(2,1)} copy(bf16[16,8,120,128]{3,2,1,0:T(8,128)(2,1)S(1)} %bitcast.35) | data formatting | bytes 7864320
  123.7 11.4 %shard_map.47 = f32[2,16,2,8,8,128]{5,4,3,2,1,0:T(8,128)} custom-call(s32[2]{0:T(128)S(1)} %add_convert_fusion.flags, f32[2,16,8,8,128]{4,3,2,1,0:T(8,128)S(1)} %get-tuple-element.11.first, f32[2,16,8,8,128]{4,3,2,1,0:T(8,128)S(1)} %get-tuple-element.12.second, f32[2,16,8,8,128]{4,3,2,1,0:T(8,128)} %collective-permute-done.7.x_back, ...), custom_call_target="tpu_custom_call" | custom-call | tf_op jit(solution)/shard_map/pallas_call | solution.py:272
  135.2 56.9 %all_to_all.11 = f32[32,2,8,8,128]{4,3,2,1,0:T(8,128)S(1)} all-to-all(f32[32,2,8,8,128]{4,3,2,1,0:T(8,128)} %bitcast.42), channel_id=1, replica_groups=mesh['half'=2,'column'=4,'core'=2,'row'=4,'run'=4] {'half','row','run'}, dimensions={0} | all-to-all | bytes 4194304 | tf_op jit(solution)/shard_map/all_to_all | solution.py:281
  192.0 1.6 copy.33
  (25 shorter events, 0.5 us)
Async XLA Ops:
  65.4 3.4 %copy-start.1 = (s32[2,64,32]{1,2,0:T(8,128)S(1)}, s32[2,64,32]{1,2,0:T(8,128)}, u32[]{:S(2)}) copy-start(s32[2,64,32]{1,2,0:T(8,128)} %param.6) | copy-start | bytes 49156
  67.0 18.7 %collective-permute-start = (f32[2,16,8,8,128]{4,2,1,0,3:T(8,128)}, f32[2,16,8,8,128]{4,2,1,0,3:T(8,128)}, u32[]{:S(2)}, u32[]{:S(2)}) collective-permute-start(f32[2,16,8,8,128]{4,2,1,0,3:T(8,128)} %get-tuple-element.21), channel_id=1, source_target_pairs={{0,16},{1,17},{2,18},{3,19},{4,20},{5,21},{6,22},{7,23},{8,24},{9,... | collective-permute-start | bytes 3145736 | tf_op jit(solution)/shard_map/ppermute | solution.py:68
  67.0 21.5 %collective-permute-start.1 = (f32[2,16,8,8,128]{4,2,1,0,3:T(8,128)}, f32[2,16,8,8,128]{4,2,1,0,3:T(8,128)}, u32[]{:S(2)}, u32[]{:S(2)}) collective-permute-start(f32[2,16,8,8,128]{4,2,1,0,3:T(8,128)} %get-tuple-element.22), channel_id=1, source_target_pairs={{0,112},{1,113},{2,114},{3,115},{4,116},{5,117},{6,118},{7,119},{8... | collective-permute-start | bytes 3145736 | tf_op jit(solution)/shard_map/ppermute | solution.py:68
  69.5 10.8 %collective-permute-start.2 = (f32[2,16,2,8,128]{4,2,1,0,3:T(2,128)S(1)}, f32[2,16,2,8,128]{4,2,1,0,3:T(2,128)S(1)}, u32[]{:S(2)}, u32[]{:S(2)}) collective-permute-start(f32[2,16,2,8,128]{4,2,1,0,3:T(2,128)S(1)} %bitcast.45), channel_id=1, source_target_pairs={{0,1},{1,2},{2,3},{3,128},{4,5},{5,6},{6,7},{7,132},{8,9},{9,10},{... | collective-permute-start | bytes 786440 | tf_op jit(solution)/shard_map/ppermute | solution.py:68
  70.0 8.5 %collective-permute-start.6 = (f32[2,8,8]{2,1,0:T(8,128)S(1)}, f32[2,8,8]{2,1,0:T(8,128)S(1)}, u32[]{:S(2)}, u32[]{:S(2)}) collective-permute-start(f32[2,8,8]{2,1,0:T(8,128)S(1)} %bitcast.47), channel_id=1, source_target_pairs={{0,128},{1,129},{2,130},{3,131},{4,132},{5,133},{6,134},{7,135},{8... | collective-permute-start | bytes 1544 | tf_op jit(solution)/shard_map/ppermute | solution.py:68
  73.2 12.3 %collective-permute-start.3 = (f32[2,16,2,8,128]{4,2,1,0,3:T(2,128)S(1)}, f32[2,16,2,8,128]{4,2,1,0,3:T(2,128)S(1)}, u32[]{:S(2)}, u32[]{:S(2)}) collective-permute-start(f32[2,16,2,8,128]{4,2,1,0,3:T(2,128)S(1)} %bitcast.44), channel_id=1, source_target_pairs={{0,131},{1,0},{2,1},{3,2},{4,135},{5,4},{6,5},{7,6},{8,139},{9,8},... | collective-permute-start | bytes 786440 | tf_op jit(solution)/shard_map/ppermute | solution.py:68
  78.5 12.8 %collective-permute-start.5 = (f32[2,16,2,8,128]{4,3,2,1,0:T(8,128)}, f32[2,16,2,8,128]{4,3,2,1,0:T(8,128)S(1)}, u32[]{:S(2)}, u32[]{:S(2)}) collective-permute-start(f32[2,16,2,8,128]{4,3,2,1,0:T(8,128)} %get-tuple-element.17), channel_id=1, source_target_pairs={{0,12},{1,13},{2,14},{3,15},{4,0},{5,1},{6,2},{7,3},{8,4},{9,5},{1... | collective-permute-start | bytes 786440 | tf_op jit(solution)/shard_map/ppermute | solution.py:68
  80.3 11.0 %collective-permute-start.4 = (f32[2,16,2,8,128]{4,3,2,1,0:T(8,128)}, f32[2,16,2,8,128]{4,3,2,1,0:T(8,128)S(1)}, u32[]{:S(2)}, u32[]{:S(2)}) collective-permute-start(f32[2,16,2,8,128]{4,3,2,1,0:T(8,128)} %get-tuple-element.18), channel_id=1, source_target_pairs={{0,4},{1,5},{2,6},{3,7},{4,8},{5,9},{6,10},{7,11},{8,12},{9,13},{1... | collective-permute-start | bytes 786440 | tf_op jit(solution)/shard_map/ppermute | solution.py:68
  97.0 26.7 %collective-permute-start.8 = (f32[2,16,8,8,128]{4,3,2,1,0:T(8,128)S(1)}, f32[2,16,8,8,128]{4,3,2,1,0:T(8,128)S(1)}, u32[]{:S(2)}, u32[]{:S(2)}) collective-permute-start(f32[2,16,8,8,128]{4,3,2,1,0:T(8,128)S(1)} %get-tuple-element.11.first), channel_id=1, source_target_pairs={{0,112},{1,113},{2,114},{3,115},{4,116},{5,117},{6,118},{7,119},{8... | collective-permute-start | bytes 3145736 | tf_op jit(solution)/shard_map/ppermute | solution.py:68
  97.0 26.7 %collective-permute-start.7 = (f32[2,16,8,8,128]{4,3,2,1,0:T(8,128)S(1)}, f32[2,16,8,8,128]{4,3,2,1,0:T(8,128)}, u32[]{:S(2)}, u32[]{:S(2)}) collective-permute-start(f32[2,16,8,8,128]{4,3,2,1,0:T(8,128)S(1)} %get-tuple-element.12.second), channel_id=1, source_target_pairs={{0,16},{1,17},{2,18},{3,19},{4,20},{5,21},{6,22},{7,23},{8,24},{9,... | collective-permute-start | bytes 3145736 | tf_op jit(solution)/shard_map/ppermute | solution.py:68
  97.5 10.3 %collective-permute-start.9 = (f32[2,16,2,8,128]{4,3,2,1,0:T(8,128)S(1)}, f32[2,16,2,8,128]{4,3,2,1,0:T(8,128)S(1)}, u32[]{:S(2)}, u32[]{:S(2)}) collective-permute-start(f32[2,16,2,8,128]{4,3,2,1,0:T(8,128)S(1)} %get-tuple-element.13), channel_id=1, source_target_pairs={{0,1},{1,2},{2,3},{3,128},{4,5},{5,6},{6,7},{7,132},{8,9},{9,10},{... | collective-permute-start | bytes 786440 | tf_op jit(solution)/shard_map/ppermute | solution.py:68
  97.6 26.1 %collective-permute-start.10 = (f32[2,16,2,8,128]{4,3,2,1,0:T(8,128)}, f32[2,16,2,8,128]{4,3,2,1,0:T(8,128)}, u32[]{:S(2)}, u32[]{:S(2)}) collective-permute-start(f32[2,16,2,8,128]{4,3,2,1,0:T(8,128)} %get-tuple-element.14), channel_id=1, source_target_pairs={{0,131},{1,0},{2,1},{3,2},{4,135},{5,4},{6,5},{7,6},{8,139},{9,8},... | collective-permute-start | bytes 786440 | tf_op jit(solution)/shard_map/ppermute | solution.py:68
  100.8 22.9 %collective-permute-start.11 = (f32[2,16,2,8,128]{4,3,2,1,0:T(8,128)}, f32[2,16,2,8,128]{4,3,2,1,0:T(8,128)}, u32[]{:S(2)}, u32[]{:S(2)}) collective-permute-start(f32[2,16,2,8,128]{4,3,2,1,0:T(8,128)} %get-tuple-element.15), channel_id=1, source_target_pairs={{0,4},{1,5},{2,6},{3,7},{4,8},{5,9},{6,10},{7,11},{8,12},{9,13},{1... | collective-permute-start | bytes 786440 | tf_op jit(solution)/shard_map/ppermute | solution.py:68
  107.8 15.9 %collective-permute-start.12 = (f32[2,16,2,8,128]{4,3,2,1,0:T(8,128)}, f32[2,16,2,8,128]{4,3,2,1,0:T(8,128)}, u32[]{:S(2)}, u32[]{:S(2)}) collective-permute-start(f32[2,16,2,8,128]{4,3,2,1,0:T(8,128)} %get-tuple-element.16), channel_id=1, source_target_pairs={{0,12},{1,13},{2,14},{3,15},{4,0},{5,1},{6,2},{7,3},{8,4},{9,5},{1... | collective-permute-start | bytes 786440 | tf_op jit(solution)/shard_map/ppermute | solution.py:68
  121.1 2.7 %copy-start = (bf16[8,128,128]{2,1,0:T(8,128)(2,1)S(1)}, bf16[8,128,128]{2,1,0:T(8,128)(2,1)}, u32[]{:S(2)}) copy-start(bf16[8,128,128]{2,1,0:T(8,128)(2,1)} %constant.81.clone.selector) | copy-start | bytes 786436

commit v2 on v1

v2 whole, which is shorter than its diff:
```python
import functools
import math

import jax
import jax.numpy as jnp
import numpy as np
from jax import lax
from jax.experimental import pallas as pl
from jax.experimental.pallas import tpu as pltpu
from jax.sharding import Mesh, PartitionSpec as P

MA = 16
MB = 16
MC = 8
LDEG = 7
BASIS_SIZE = 120
LANES = MB * MC
LOW_A = LDEG + 1
PAD = 128
CFL = 0.04
DTC = 0.2
HALF = 0.5 * CFL
CX = HALF * 2.0 * math.sqrt(MA)
CY = HALF * 2.0 * math.sqrt(MB)
CZ = HALF * 2.0 * math.sqrt(MC)
CENTER = 2.0 * (CX + CY + CZ)
ROWS = 8
COLS = 8
GROUP = 16
BLOCKS = 32

AXES = ("half", "column", "core", "row", "run")
SIZES = (2, 4, 2, 4, 4)


def pairs(move):
    out = []
    for source in np.ndindex(*SIZES):
        target = move(*source)
        out.append((int(np.ravel_multi_index(source, SIZES)), int(np.ravel_multi_index(target, SIZES))))
    return out


def outer():
    def move(half, column, core, row, run):
        place = (column * 2 + core + (1 if core else -1)) % 8
        return (half, place // 2, place % 2, row, run)

    return pairs(move)


def inner():
    return pairs(lambda half, column, core, row, run: (half, column, 1 - core, row, run))


def along_y(by):
    def move(half, column, core, row, run):
        place = (half * 4 + run + by) % 8
        return (place // 4, column, core, row, place % 4)

    return pairs(move)


def along_z(by):
    return pairs(lambda half, column, core, row, run: (half, column, core, (row + by) % 4, run))


def other_half():
    return pairs(lambda half, column, core, row, run: (1 - half, column, core, row, run))


def send(value, route):
    return lax.ppermute(value, AXES, route)


def ladder_rows():
    lane = lax.broadcasted_iota(jnp.int32, (COLS, LANES), 1)
    b = lane // MC
    c = lane % MC
    b_low = HALF * jnp.sqrt(b.astype(jnp.float32))
    b_high = jnp.where(b < MB - 1, HALF * jnp.sqrt((b + 1).astype(jnp.float32)), 0.0)
    c_low = HALF * jnp.sqrt(c.astype(jnp.float32))
    c_high = jnp.where(c < MC - 1, HALF * jnp.sqrt((c + 1).astype(jnp.float32)), 0.0)
    return b_low, b_high, c_low, c_high


def advance(swap, steps, here, beside, beyond, y_back, y_next, z_back, z_next, open_cells, put):
    b_low, b_high, c_low, c_high = ladder_rows()
    depth = lax.broadcasted_iota(jnp.int32, (COLS, LANES), 0)
    at_start = depth == 0
    at_end = depth == COLS - 1

    def block(g, carry):
        far = g if swap is None else jnp.where(swap, 1 - g, g)
        for y in range(ROWS):

            def sides(a):
                near = beside[g, a, y]
                other = beyond[far, a, y]
                return near - other, near + other

            is_open = open_cells[g, y]
            before = None
            now = sides(0)
            for a in range(MA):
                after = sides(a + 1) if a + 1 < MA else None
                f = here[g, a, y]
                yb = here[g, a, y - 1] if y > 0 else y_back[g, a]
                yn = here[g, a, y + 1] if y + 1 < ROWS else y_next[g, a]
                zb = jnp.where(at_start, z_back[g, a, y : y + 1, :], pltpu.roll(f, 1, 0))
                zn = jnp.where(at_end, z_next[g, a, y : y + 1, :], pltpu.roll(f, COLS - 1, 0))
                dy = yn - yb
                dz = zn - zb
                change = CX * (now[1] + (yn + yb)) + CZ * (zn + zb) - CENTER * f
                if before is not None:
                    change = change - steps[a] * before
                if after is not None:
                    change = change - steps[a + 1] * after[0]
                change = change - b_low * pltpu.roll(dy, MC, 1)
                change = change - b_high * pltpu.roll(dy, LANES - MC, 1)
                change = change - c_low * pltpu.roll(dz, 1, 1)
                change = change - c_high * pltpu.roll(dz, LANES - 1, 1)
                put(g, a, y, f + is_open * change)
                before = now[0]
                now = after
        return carry

    lax.fori_loop(0, 2, block, 0)


def put_edges(g, a, y, value, out_y0, out_y7, out_z0, out_z7):
    if y == 0:
        out_y0[g, a] = value
    if y == ROWS - 1:
        out_y7[g, a] = value
    out_z0[g, a, y : y + 1, :] = value[0:1]
    out_z7[g, a, y : y + 1, :] = value[COLS - 1 : COLS]


def split_kernel(state, out_outer, out_inner, *edges):
    def block(index, carry):
        g = index // MA
        a = index % MA
        for which, out in enumerate((out_outer, out_inner)):
            for y in range(ROWS):
                value = state[g, a, which, y]
                out[g, a, y] = value
                put_edges(g, a, y, value, *[edge.at[which] for edge in edges])
        return carry

    lax.fori_loop(0, 2 * MA, block, 0)


def open_table(mine, theirs, table):
    half = lax.axis_index("half")
    cols = pl.ds(pl.multiple_of(lax.axis_index("row") * COLS, COLS), COLS)
    first_row = (half * 4 + lax.axis_index("run")) * ROWS
    for own, source in enumerate((theirs, mine)):
        g = half if own else 1 - half
        for which, plane in enumerate(plane_order()):
            cells = jnp.where(source[plane, cols, :] != 0, 0.0, 1.0)
            wide = jnp.concatenate([cells, cells], 1)
            wide = pltpu.roll(wide, LANES - first_row, 1)
            for y in range(ROWS):
                table[which, g, y] = jnp.broadcast_to(wide[:, y : y + 1], (COLS, LANES))


def both_planes(planes, beyond, faces, open_cells, put):
    column = lax.axis_index("column")
    core = lax.axis_index("core")
    sign = jnp.where(core == 0, 1.0, -1.0).astype(jnp.float32)
    wraps = ((column == 0) & (core == 0)) | ((column == 3) & (core == 1))
    for which in range(2):
        steps = [(1 - 2 * which) * HALF * math.sqrt(a) * sign for a in range(MA)]
        advance(
            wraps if which == 0 else None, steps, planes[which], planes[1 - which], beyond[which],
            *[face.at[which] for face in faces], open_cells.at[which], functools.partial(put, which),
        )


def first_kernel(
    outer_plane, inner_plane, outer_beyond, inner_beyond, y_back, y_next, z_back, z_next,
    mine, theirs, out_outer, out_inner, open_cells, *edges,
):
    open_table(mine, theirs, open_cells)

    def put(which, g, a, y, value):
        (out_outer, out_inner)[which][g, a, y] = value
        put_edges(g, a, y, value, *[edge.at[which] for edge in edges])

    both_planes(
        (outer_plane, inner_plane), (outer_beyond, inner_beyond), (y_back, y_next, z_back, z_next),
        open_cells, put,
    )


def tile_of(half, row):
    return half, slice(None), slice(None), pl.ds(row * COLS, COLS)


def plane_order():
    core = lax.axis_index("core")
    return core, 1 - core


def gather_blocks(field, blocks, arrived):
    copies = []
    for which, plane in enumerate(plane_order()):
        for half in range(2):
            for row in range(4):
                copies.append(
                    pltpu.make_async_copy(
                        field.at[plane].at[tile_of(half, row)],
                        blocks.at[half, row, :, which],
                        arrived.at[which, half, row],
                    )
                )
    for copy in copies:
        copy.start()
    for copy in copies:
        copy.wait()


def scatter_blocks(blocks, field, arrived):
    copies = []
    for which, plane in enumerate(plane_order()):
        for half in range(2):
            for row in range(4):
                copies.append(
                    pltpu.make_async_copy(
                        blocks.at[half, row, :, which],
                        field.at[plane].at[tile_of(half, row)],
                        arrived.at[which, half, row],
                    )
                )
    for copy in copies:
        copy.start()
    for copy in copies:
        copy.wait()


def three_parts(value):
    high = value.astype(jnp.bfloat16)
    rest = value - high.astype(jnp.float32)
    middle = rest.astype(jnp.bfloat16)
    low = (rest - middle.astype(jnp.float32)).astype(jnp.bfloat16)
    return high, middle, low


def second_kernel(
    outer_plane, inner_plane, outer_beyond, inner_beyond, y_back, y_next, z_back, z_next,
    open_cells, selector, weights, out, low, factors,
):
    def put(which, g, a, y, value):
        out[g, a, which, y] = value

    both_planes(
        (outer_plane, inner_plane), (outer_beyond, inner_beyond), (y_back, y_next, z_back, z_next),
        open_cells, put,
    )
    cells = 2 * 2 * ROWS * COLS
    lane = lax.broadcasted_iota(jnp.int32, (cells, LANES), 1)

    def plane(a):
        parts = [out[g, a, p].reshape(ROWS * COLS, LANES) for g in range(2) for p in range(2)]
        return jnp.concatenate(parts, 0)

    picked = jnp.zeros((PAD, cells), jnp.float32)
    for a in range(0, LOW_A, 2):
        paired = jnp.where(lane < LANES // 2, plane(a), pltpu.roll(plane(a + 1), LANES // 2, 1))
        for part in three_parts(paired):
            picked = picked + lax.dot_general(
                selector[a // 2], part, (((1,), (1,)), ((), ())), preferred_element_type=jnp.float32
            )
    low[...] = picked

    rate = jnp.zeros((BASIS_SIZE, cells), jnp.float32)
    values = low[0:BASIS_SIZE]
    for step in range(0, BASIS_SIZE, GROUP):
        count = min(GROUP, BASIS_SIZE - step)
        slot = factors.at[step // GROUP % 2]
        for i in range(0, count, 2):
            pair = [values * low[step + i + n : step + i + n + 1, :] for n in range(2)]
            slot[i * BASIS_SIZE : (i + 2) * BASIS_SIZE, :] = jnp.concatenate(pair, 0).astype(jnp.bfloat16)
        rate = rate + jnp.dot(
            weights[:, step * BASIS_SIZE : (step + count) * BASIS_SIZE],
            slot[0 : count * BASIS_SIZE, :],
            preferred_element_type=jnp.float32,
        )
    rate = jnp.concatenate([rate, jnp.zeros((PAD - BASIS_SIZE, cells), jnp.float32)], 0)
    rate_parts = three_parts(jnp.transpose(DTC * rate))
    for a in range(0, LOW_A, 2):
        lifted = jnp.zeros((cells, LANES), jnp.float32)
        for part in rate_parts:
            lifted = lifted + jnp.dot(part, selector[a // 2], preferred_element_type=jnp.float32)
        halves = (
            jnp.where(lane < LANES // 2, lifted, 0.0),
            jnp.where(lane < LANES // 2, pltpu.roll(lifted, LANES // 2, 1), 0.0),
        )
        for n, value in enumerate(halves):
            for g in range(2):
                for p in range(2):
                    at = (g * 2 + p) * ROWS * COLS
                    block = value[at : at + ROWS * COLS].reshape(ROWS, COLS, LANES)
                    out[g, a + n, p] = out[g, a + n, p] + block


def low_selector():
    rank = 0
    table = np.zeros((LOW_A // 2, PAD, LANES), np.float32)
    for a in range(MA):
        for b in range(MB):
            for c in range(MC):
                if a + b + c <= LDEG:
                    table[a // 2, rank, a % 2 * (LANES // 2) + b * MC + c] = 1.0
                    rank += 1
    return jnp.asarray(table, jnp.bfloat16)


VMEM = pl.BlockSpec(memory_space=pltpu.VMEM)
PARAMS = pltpu.CompilerParams(vmem_limit_bytes=16 << 20)
HBM = pl.BlockSpec(memory_space=pltpu.HBM)
COPY_SEMS = [pltpu.SemaphoreType.DMA((2, 2, 4))]


def f32(*shape):
    return jax.ShapeDtypeStruct(shape, jnp.float32)


PLANE = f32(2, MA, ROWS, COLS, LANES)
EDGES = f32(2, 2, MA, ROWS, LANES)


def surroundings(outer_plane, inner_plane, edges):
    y0, y7, z0, z7 = edges
    outer_beyond = send(outer_plane, outer())
    inner_beyond = send(inner_plane, inner())
    y_back = send(y7, along_y(1))
    y_next = send(y0, along_y(-1))
    z_back = send(z7, along_z(1))
    z0, inner_beyond = lax.optimization_barrier((z0, inner_beyond))
    z_next = send(z0, along_z(-1))
    return outer_beyond, inner_beyond, y_back, y_next, z_back, z_next


def call(kernel, out_shape, *operands, operand_space=VMEM, out_space=VMEM, scratch=()):
    single = not isinstance(out_shape, tuple)
    return pl.pallas_call(
        kernel,
        out_shape=out_shape,
        in_specs=[operand_space] * len(operands),
        out_specs=out_space if single else (out_space,) * len(out_shape),
        scratch_shapes=scratch,
        compiler_params=PARAMS,
    )(*operands)


def exchange(blocks):
    return lax.all_to_all(blocks, ("half", "row", "run"), 0, 0, tiled=True)


def body(field, kernel_table, obstacles):
    mine = obstacles.transpose(0, 2, 1)
    theirs = send(mine, other_half())
    tiles = f32(2, 4, 4, 2, ROWS, COLS, LANES)
    tiled = (2, 2, 4, ROWS, 4 * COLS, LANES)
    blocks = call(gather_blocks, tiles, field.reshape(tiled), operand_space=HBM, scratch=COPY_SEMS)
    state = exchange(blocks.reshape(BLOCKS, 2, ROWS, COLS, LANES))
    state, theirs = lax.optimization_barrier((state, theirs))

    outer_plane, inner_plane, *edges = call(
        split_kernel, (PLANE,) * 2 + (EDGES,) * 4, state.reshape(2, MA, 2, ROWS, COLS, LANES)
    )
    around = surroundings(outer_plane, inner_plane, edges)
    outer_plane, inner_plane, open_cells, *edges = call(
        first_kernel, (PLANE,) * 2 + (f32(2, 2, ROWS, COLS, LANES),) + (EDGES,) * 4,
        outer_plane, inner_plane, *around, mine, theirs,
    )
    around = surroundings(outer_plane, inner_plane, edges)
    cells = 2 * 2 * ROWS * COLS
    state = call(
        second_kernel, f32(2, MA, 2, ROWS, COLS, LANES),
        outer_plane, inner_plane, *around, open_cells, low_selector(), kernel_table.T,
        scratch=[
            pltpu.VMEM((PAD, cells), jnp.float32),
            pltpu.VMEM((2, GROUP * BASIS_SIZE, cells), jnp.bfloat16),
        ],
    )
    back = exchange(state.reshape(BLOCKS, 2, ROWS, COLS, LANES))
    result = call(
        scatter_blocks, f32(*tiled), back.reshape(tiles.shape), out_space=HBM, scratch=COPY_SEMS
    )
    return result.reshape(2, 8 * ROWS, 4 * COLS, LANES)


def solution(mesh):
    named = Mesh(mesh.devices.reshape(SIZES), AXES)
    cells = ("half", "column", "core")
    modes = ("row", "run")
    placed = (P(cells, None, None, modes), P(), P(cells, None, None))
    return jax.shard_map(
        body, mesh=named, in_specs=placed, out_specs=P(cells, None, None, modes), check_vma=False
    )
```

time: 196 us -> 166 us (0.85); the launches traced: 194 us -> 166 us
  blocking collectives: 119 us -> 56.9 us
  waiting for transfers between devices: 8.83 us -> 61.1 us
  local copies, waits for them, and re-layouts: 31.6 us -> 2.92 us
  starting transfers between devices: 16.6 us -> 33.1 us
  Pallas kernels: 17 us -> 11.6 us
    all_to_all x2 -> x1, blocking collectives: 119 us -> 56.9 us  [exchange(): return lax.all_to_all(blocks, ('half', 'row', 'run'), 0, 0, tiled=True)]
    ppermute x13, waiting for transfers between devices: 8.83 us -> 61.1 us  [send(): return lax.ppermute(value, AXES, route)]
    reshape x4 -> x0, local copies, waits for them, and re-layouts: 12.3 us -> none  [the longest x1 7.7 us: body(): kernel_table.reshape(BASIS_SIZE, BASIS_SIZE, BASIS_SIZE).transpose(2, 0, 1)]
    all_to_all x0 -> x1, starting transfers between devices: none -> 11.6 us  [exchange(): return lax.all_to_all(blocks, ('half', 'row', 'run'), 0, 0, tiled=True)]
    squeeze x4 -> x0, local copies, waits for them, and re-layouts: 7.06 us -> none  [the longest x2 4.39 us: body(): second = state[:, :, 1]]
    ppermute x4 -> x0, local copies, waits for them, and re-layouts: 5.93 us -> none  [send(): return lax.ppermute(value, AXES, route)]
    pallas_call x2 -> x5, Pallas kernels: 17 us -> 11.6 us  [call(): pl.pallas_call(kernel, out_shape=out_shape, in_specs=[operand_space] * le...]
    ppermute x13, starting transfers between devices: 16.6 us -> 21.5 us  [send(): return lax.ppermute(value, AXES, route)]
  transfers between devices with their start and end apart: 13 -> 14, of which waited for: 2 -> 7; matrix products, arithmetic and copies ran while one was open for 13% -> 0% of each run, Pallas kernels for 0% -> 0%
where the time goes in v2:
time: 166 us
  waiting for transfers between devices  61.1 us (37%)
  blocking collectives  56.9 us (34%)
  starting transfers between devices  33.1 us (20%)
  Pallas kernels  11.6 us (7%)
  local copies, waits for them, and re-layouts  2.92 us (2%)
    ppermute x13, waiting for transfers between devices, send(): return lax.ppermute(value, AXES, route)  61.1 us
    all_to_all x1, blocking collectives, exchange(): return lax.all_to_all(blocks, ('half', 'row', 'run'), 0, 0, tiled=True)  56.9 us
    ppermute x13, starting transfers between devices, send(): return lax.ppermute(value, AXES, route)  21.5 us
    all_to_all x1, starting transfers between devices, exchange(): return lax.all_to_all(blocks, ('half', 'row', 'run'), 0, 0, tiled=True)  11.6 us
    pallas_call x5, Pallas kernels, call(): pl.pallas_call(kernel, out_shape=out_shape, in_specs=[operand_space] * le...  11.6 us
  transfers between devices with their start and end apart: 14, of which 7 were waited for; matrix products, arithmetic and copies ran while one was open for 0% of the time, Pallas kernels for 0%

profile of v2, /device:TPU:6, one launch (start us, length us, event | category | flops | bytes accessed | tf_op | source)
XLA Modules:
  0.0 165.8 jit_solution(6001662291111437728)
XLA Ops:
  0.0 1.6 copy-done.2
  1.6 0.5 shard_map.46
  2.1 0.0 copy-start
  2.1 1.3 copy-done
  3.4 11.6 %all-to-all-start = ((f32[32,2,8,8,128]{4,3,2,1,0:T(8,128)}), f32[32,2,8,8,128]{4,3,2,1,0:T(8,128)S(1)}, u32[]{:S(2)}, u32[]{:S(2)}) async-start(f32[32,2,8,8,128]{4,3,2,1,0:T(8,128)} %bitcast.10), calls=%async_computation | async-start | bytes 4194304 | tf_op jit(solution)/shard_map/all_to_all | solution.py:359
  15.0 5.8 %collective-permute-start = (s32[2,32,64]{2,1,0:T(8,128)S(1)}, s32[2,32,64]{2,1,0:T(8,128)S(1)}, u32[]{:S(2)}, u32[]{:S(2)}) collective-permute-start(s32[2,32,64]{2,1,0:T(8,128)S(1)} %bitcast.14), channel_id=1, source_target_pairs={{0,128},{1,129},{2,130},{3,131},{4,132},{5,133},{6,134},{7,135},{8... | collective-permute-start | bytes 49160 | tf_op jit(solution)/shard_map/ppermute | solution.py:73
  20.8 46.5 %collective-permute-done.theirs = s32[2,32,64]{2,1,0:T(8,128)S(1)} collective-permute-done((s32[2,32,64]{2,1,0:T(8,128)S(1)}, s32[2,32,64]{2,1,0:T(8,128)S(1)}, u32[]{:S(2)}, u32[]{:S(2)}) %collective-permute-start) | collective-permute-done | bytes 16416 | tf_op jit(solution)/shard_map/ppermute | solution.py:73
  67.3 0.0 all-to-all-done
  67.3 0.7 shard_map.47
  68.0 0.1 collective-permute-start.2
  68.1 0.9 collective-permute-start.1
  69.0 0.6 collective-permute-start.3
  69.6 2.7 %collective-permute-start.4 = (f32[2,2,16,8,128]{4,3,2,1,0:T(8,128)S(1)}, f32[2,2,16,8,128]{4,3,2,1,0:T(8,128)S(1)}, u32[]{:S(2)}, u32[]{:S(2)}) collective-permute-start(f32[2,2,16,8,128]{4,3,2,1,0:T(8,128)S(1)} %get-tuple-element.30), channel_id=1, source_target_pairs={{0,131},{1,0},{2,1},{3,2},{4,135},{5,4},{6,5},{7,6},{8,139},{9,8},... | collective-permute-start | bytes 786440 | tf_op jit(solution)/shard_map/ppermute | solution.py:73
  72.2 1.5 collective-permute-start.5
  73.7 1.8 %collective-permute-start.6 = (f32[2,2,16,8,128]{4,3,2,1,0:T(8,128)S(1)}, f32[2,2,16,8,128]{4,3,2,1,0:T(8,128)S(1)}, u32[]{:S(2)}, u32[]{:S(2)}) collective-permute-start(f32[2,2,16,8,128]{4,3,2,1,0:T(8,128)S(1)} %get-tuple-element.32), channel_id=1, source_target_pairs={{0,12},{1,13},{2,14},{3,15},{4,0},{5,1},{6,2},{7,3},{8,4},{9,5},{1... | collective-permute-start | bytes 786440 | tf_op jit(solution)/shard_map/ppermute | solution.py:73
  75.5 2.7 %collective-permute-done.3.y_back = f32[2,2,16,8,128]{4,3,2,1,0:T(8,128)S(1)} collective-permute-done((f32[2,2,16,8,128]{4,3,2,1,0:T(8,128)S(1)}, f32[2,2,16,8,128]{4,3,2,1,0:T(8,128)S(1)}, u32[]{:S(2)}, u32[]{:S(2)}) %collective-permute-start.3) | collective-permute-done | bytes 262176 | tf_op jit(solution)/shard_map/ppermute | solution.py:73
  78.2 0.0 collective-permute-done.4.y_next
  78.2 2.7 %collective-permute-done.5.z_back = f32[2,2,16,8,128]{4,3,2,1,0:T(8,128)S(1)} collective-permute-done((f32[2,2,16,8,128]{4,3,2,1,0:T(8,128)S(1)}, f32[2,2,16,8,128]{4,3,2,1,0:T(8,128)S(1)}, u32[]{:S(2)}, u32[]{:S(2)}) %collective-permute-start.5) | collective-permute-done | bytes 262176 | tf_op jit(solution)/shard_map/ppermute | solution.py:73
  80.9 1.5 collective-permute-done.1.outer_beyond
  82.4 2.8 %shard_map.48 = (f32[2,16,8,8,128]{4,3,2,1,0:T(8,128)S(1)}, f32[2,16,8,8,128]{4,3,2,1,0:T(8,128)S(1)}, f32[2,2,8,8,128]{4,3,2,1,0:T(8,128)S(1)}, f32[2,2,16,8,12...) custom-call(f32[2,16,8,8,128]{4,3,2,1,0:T(8,128)S(1)} %get-tuple-ele, ...), custom_call_target="tpu_custom_call" | custom-call | tf_op jit(solution)/shard_map/pallas_call | solution.py:348
  85.2 1.7 %collective-permute-start.8 = (f32[2,16,8,8,128]{4,3,2,1,0:T(8,128)S(1)}, f32[2,16,8,8,128]{4,3,2,1,0:T(8,128)S(1)}, u32[]{:S(2)}, u32[]{:S(2)}) collective-permute-start(f32[2,16,8,8,128]{4,3,2,1,0:T(8,128)S(1)} %get-tuple-element.35.inner_plane), channel_id=1, source_target_pairs={{0,16},{1,17},{2,18},{3,19},{4,20},{5,21},{6,22},{7,23},{8,24},{9,... | collective-permute-start | bytes 3145736 | tf_op jit(solution)/shard_map/ppermute | solution.py:73
  86.9 0.0 collective-permute-start.7
  86.9 0.6 collective-permute-start.9
  87.5 2.7 %collective-permute-start.10 = (f32[2,2,16,8,128]{4,3,2,1,0:T(8,128)S(1)}, f32[2,2,16,8,128]{4,3,2,1,0:T(8,128)S(1)}, u32[]{:S(2)}, u32[]{:S(2)}) collective-permute-start(f32[2,2,16,8,128]{4,3,2,1,0:T(8,128)S(1)} %get-tuple-element.39), channel_id=1, source_target_pairs={{0,131},{1,0},{2,1},{3,2},{4,135},{5,4},{6,5},{7,6},{8,139},{9,8},... | collective-permute-start | bytes 786440 | tf_op jit(solution)/shard_map/ppermute | solution.py:73
  90.2 1.5 collective-permute-start.11
  91.6 1.8 %collective-permute-start.12 = (f32[2,2,16,8,128]{4,3,2,1,0:T(8,128)S(1)}, f32[2,2,16,8,128]{4,3,2,1,0:T(8,128)S(1)}, u32[]{:S(2)}, u32[]{:S(2)}) collective-permute-start(f32[2,2,16,8,128]{4,3,2,1,0:T(8,128)S(1)} %get-tuple-element.41), channel_id=1, source_target_pairs={{0,12},{1,13},{2,14},{3,15},{4,0},{5,1},{6,2},{7,3},{8,4},{9,5},{1... | collective-permute-start | bytes 786440 | tf_op jit(solution)/shard_map/ppermute | solution.py:73
  93.4 3.2 %collective-permute-done.9.y_back = f32[2,2,16,8,128]{4,3,2,1,0:T(8,128)S(1)} collective-permute-done((f32[2,2,16,8,128]{4,3,2,1,0:T(8,128)S(1)}, f32[2,2,16,8,128]{4,3,2,1,0:T(8,128)S(1)}, u32[]{:S(2)}, u32[]{:S(2)}) %collective-permute-start.9) | collective-permute-done | bytes 262176 | tf_op jit(solution)/shard_map/ppermute | solution.py:73
  96.7 2.7 %collective-permute-done.11.z_back = f32[2,2,16,8,128]{4,3,2,1,0:T(8,128)S(1)} collective-permute-done((f32[2,2,16,8,128]{4,3,2,1,0:T(8,128)S(1)}, f32[2,2,16,8,128]{4,3,2,1,0:T(8,128)S(1)}, u32[]{:S(2)}, u32[]{:S(2)}) %collective-permute-start.11) | collective-permute-done | bytes 262176 | tf_op jit(solution)/shard_map/ppermute | solution.py:73
  99.3 1.8 %collective-permute-done.7.outer_beyond = f32[2,16,8,8,128]{4,3,2,1,0:T(8,128)S(1)} collective-permute-done((f32[2,16,8,8,128]{4,3,2,1,0:T(8,128)S(1)}, f32[2,16,8,8,128]{4,3,2,1,0:T(8,128)S(1)}, u32[]{:S(2)}, u32[]{:S(2)}) %collective-permute-start.7) | collective-permute-done | bytes 1048608 | tf_op jit(solution)/shard_map/ppermute | solution.py:73
  101.2 6.2 %shard_map.49 = f32[2,16,2,8,8,128]{5,4,3,2,1,0:T(8,128)S(1)} custom-call(f32[2,16,8,8,128]{4,3,2,1,0:T(8,128)S(1)} %get-tuple-element.34.outer_plane, f32[2,16,8,8,128]{4,3,2,1,0:T(8,128)S(1)} %get-tuple-element.35.inner_plane, f32[2,16,8,8,128]{4,3,2,1,0:T(8,128)S(1)} %collective-permute-done.7.outer_beyond, ...), custom_call_target="tpu_custom_call" | custom-call | tf_op jit(solution)/shard_map/pallas_call | solution.py:348
  107.3 56.9 %all_to_all.10 = f32[32,2,8,8,128]{4,3,2,1,0:T(8,128)S(1)} all-to-all(f32[32,2,8,8,128]{4,3,2,1,0:T(8,128)S(1)} %bitcast.8), channel_id=1, replica_groups=mesh['half'=2,'column'=4,'core'=2,'row'=4,'run'=4] {'half','row','run'}, dimensions={0} | all-to-all | bytes 4194304 | tf_op jit(solution)/shard_map/all_to_all | solution.py:359
  164.3 1.4 shard_map.50
  (12 shorter events, 0.0 us)
Async XLA Ops:
  0.0 1.6 copy-start.2
  2.1 1.3 copy-start
  3.4 11.6 %copy-start.4 = (s32[2,64,32]{1,2,0:T(8,128)S(1)}, s32[2,64,32]{1,2,0:T(8,128)}, u32[]{:S(2)}) copy-start(s32[2,64,32]{1,2,0:T(8,128)} %param.6) | copy-start | bytes 49156
  3.4 63.9 %all-to-all-start = ((f32[32,2,8,8,128]{4,3,2,1,0:T(8,128)}), f32[32,2,8,8,128]{4,3,2,1,0:T(8,128)S(1)}, u32[]{:S(2)}, u32[]{:S(2)}) async-start(f32[32,2,8,8,128]{4,3,2,1,0:T(8,128)} %bitcast.10), calls=%async_computation | async-start | bytes 4194304 | tf_op jit(solution)/shard_map/all_to_all | solution.py:359
  15.0 52.3 %collective-permute-start = (s32[2,32,64]{2,1,0:T(8,128)S(1)}, s32[2,32,64]{2,1,0:T(8,128)S(1)}, u32[]{:S(2)}, u32[]{:S(2)}) collective-permute-start(s32[2,32,64]{2,1,0:T(8,128)S(1)} %bitcast.14), channel_id=1, source_target_pairs={{0,128},{1,129},{2,130},{3,131},{4,132},{5,133},{6,134},{7,135},{8... | collective-permute-start | bytes 49160 | tf_op jit(solution)/shard_map/ppermute | solution.py:73
  68.0 5.7 %collective-permute-start.2 = (f32[2,16,8,8,128]{4,3,2,1,0:T(8,128)S(1)}, f32[2,16,8,8,128]{4,3,2,1,0:T(8,128)S(1)}, u32[]{:S(2)}, u32[]{:S(2)}) collective-permute-start(f32[2,16,8,8,128]{4,3,2,1,0:T(8,128)S(1)} %get-tuple-element.26.inner_plane), channel_id=1, source_target_pairs={{0,16},{1,17},{2,18},{3,19},{4,20},{5,21},{6,22},{7,23},{8,24},{9,... | collective-permute-start | bytes 3145736 | tf_op jit(solution)/shard_map/ppermute | solution.py:73
  68.1 14.3 %collective-permute-start.1 = (f32[2,16,8,8,128]{4,3,2,1,0:T(8,128)S(1)}, f32[2,16,8,8,128]{4,3,2,1,0:T(8,128)S(1)}, u32[]{:S(2)}, u32[]{:S(2)}) collective-permute-start(f32[2,16,8,8,128]{4,3,2,1,0:T(8,128)S(1)} %get-tuple-element.25.outer_plane), channel_id=1, source_target_pairs={{0,112},{1,113},{2,114},{3,115},{4,116},{5,117},{6,118},{7,119},{8... | collective-permute-start | bytes 3145736 | tf_op jit(solution)/shard_map/ppermute | solution.py:73
  69.0 9.2 %collective-permute-start.3 = (f32[2,2,16,8,128]{4,3,2,1,0:T(8,128)S(1)}, f32[2,2,16,8,128]{4,3,2,1,0:T(8,128)S(1)}, u32[]{:S(2)}, u32[]{:S(2)}) collective-permute-start(f32[2,2,16,8,128]{4,3,2,1,0:T(8,128)S(1)} %get-tuple-element.29), channel_id=1, source_target_pairs={{0,1},{1,2},{2,3},{3,128},{4,5},{5,6},{6,7},{7,132},{8,9},{9,10},{... | collective-permute-start | bytes 786440 | tf_op jit(solution)/shard_map/ppermute | solution.py:73
  69.6 8.6 %collective-permute-start.4 = (f32[2,2,16,8,128]{4,3,2,1,0:T(8,128)S(1)}, f32[2,2,16,8,128]{4,3,2,1,0:T(8,128)S(1)}, u32[]{:S(2)}, u32[]{:S(2)}) collective-permute-start(f32[2,2,16,8,128]{4,3,2,1,0:T(8,128)S(1)} %get-tuple-element.30), channel_id=1, source_target_pairs={{0,131},{1,0},{2,1},{3,2},{4,135},{5,4},{6,5},{7,6},{8,139},{9,8},... | collective-permute-start | bytes 786440 | tf_op jit(solution)/shard_map/ppermute | solution.py:73
  72.2 8.6 %collective-permute-start.5 = (f32[2,2,16,8,128]{4,3,2,1,0:T(8,128)S(1)}, f32[2,2,16,8,128]{4,3,2,1,0:T(8,128)S(1)}, u32[]{:S(2)}, u32[]{:S(2)}) collective-permute-start(f32[2,2,16,8,128]{4,3,2,1,0:T(8,128)S(1)} %get-tuple-element.31), channel_id=1, source_target_pairs={{0,4},{1,5},{2,6},{3,7},{4,8},{5,9},{6,10},{7,11},{8,12},{9,13},{1... | collective-permute-start | bytes 786440 | tf_op jit(solution)/shard_map/ppermute | solution.py:73
  73.7 27.5 %copy-start.1 = (bf16[14400,120]{0,1:T(8,128)(2,1)S(1)}, bf16[14400,120]{0,1:T(8,128)(2,1)}, u32[]{:S(2)}) copy-start(bf16[14400,120]{0,1:T(8,128)(2,1)} %param.5) | copy-start | bytes 10368004
  73.7 27.5 %copy-start.3 = (bf16[4,128,128]{2,1,0:T(8,128)(2,1)S(1)}, bf16[4,128,128]{2,1,0:T(8,128)(2,1)}, u32[]{:S(2)}) copy-start(bf16[4,128,128]{2,1,0:T(8,128)(2,1)} %constant.2.clone.selector) | copy-start | bytes 393220
  73.7 8.7 %collective-permute-start.6 = (f32[2,2,16,8,128]{4,3,2,1,0:T(8,128)S(1)}, f32[2,2,16,8,128]{4,3,2,1,0:T(8,128)S(1)}, u32[]{:S(2)}, u32[]{:S(2)}) collective-permute-start(f32[2,2,16,8,128]{4,3,2,1,0:T(8,128)S(1)} %get-tuple-element.32), channel_id=1, source_target_pairs={{0,12},{1,13},{2,14},{3,15},{4,0},{5,1},{6,2},{7,3},{8,4},{9,5},{1... | collective-permute-start | bytes 786440 | tf_op jit(solution)/shard_map/ppermute | solution.py:73
  85.2 6.4 %collective-permute-start.8 = (f32[2,16,8,8,128]{4,3,2,1,0:T(8,128)S(1)}, f32[2,16,8,8,128]{4,3,2,1,0:T(8,128)S(1)}, u32[]{:S(2)}, u32[]{:S(2)}) collective-permute-start(f32[2,16,8,8,128]{4,3,2,1,0:T(8,128)S(1)} %get-tuple-element.35.inner_plane), channel_id=1, source_target_pairs={{0,16},{1,17},{2,18},{3,19},{4,20},{5,21},{6,22},{7,23},{8,24},{9,... | collective-permute-start | bytes 3145736 | tf_op jit(solution)/shard_map/ppermute | solution.py:73
  86.9 14.2 %collective-permute-start.7 = (f32[2,16,8,8,128]{4,3,2,1,0:T(8,128)S(1)}, f32[2,16,8,8,128]{4,3,2,1,0:T(8,128)S(1)}, u32[]{:S(2)}, u32[]{:S(2)}) collective-permute-start(f32[2,16,8,8,128]{4,3,2,1,0:T(8,128)S(1)} %get-tuple-element.34.outer_plane), channel_id=1, source_target_pairs={{0,112},{1,113},{2,114},{3,115},{4,116},{5,117},{6,118},{7,119},{8... | collective-permute-start | bytes 3145736 | tf_op jit(solution)/shard_map/ppermute | solution.py:73
  86.9 9.7 %collective-permute-start.9 = (f32[2,2,16,8,128]{4,3,2,1,0:T(8,128)S(1)}, f32[2,2,16,8,128]{4,3,2,1,0:T(8,128)S(1)}, u32[]{:S(2)}, u32[]{:S(2)}) collective-permute-start(f32[2,2,16,8,128]{4,3,2,1,0:T(8,128)S(1)} %get-tuple-element.38), channel_id=1, source_target_pairs={{0,1},{1,2},{2,3},{3,128},{4,5},{5,6},{6,7},{7,132},{8,9},{9,10},{... | collective-permute-start | bytes 786440 | tf_op jit(solution)/shard_map/ppermute | solution.py:73
  87.5 9.1 %collective-permute-start.10 = (f32[2,2,16,8,128]{4,3,2,1,0:T(8,128)S(1)}, f32[2,2,16,8,128]{4,3,2,1,0:T(8,128)S(1)}, u32[]{:S(2)}, u32[]{:S(2)}) collective-permute-start(f32[2,2,16,8,128]{4,3,2,1,0:T(8,128)S(1)} %get-tuple-element.39), channel_id=1, source_target_pairs={{0,131},{1,0},{2,1},{3,2},{4,135},{5,4},{6,5},{7,6},{8,139},{9,8},... | collective-permute-start | bytes 786440 | tf_op jit(solution)/shard_map/ppermute | solution.py:73
  90.2 9.1 %collective-permute-start.11 = (f32[2,2,16,8,128]{4,3,2,1,0:T(8,128)S(1)}, f32[2,2,16,8,128]{4,3,2,1,0:T(8,128)S(1)}, u32[]{:S(2)}, u32[]{:S(2)}) collective-permute-start(f32[2,2,16,8,128]{4,3,2,1,0:T(8,128)S(1)} %get-tuple-element.40), channel_id=1, source_target_pairs={{0,4},{1,5},{2,6},{3,7},{4,8},{5,9},{6,10},{7,11},{8,12},{9,13},{1... | collective-permute-start | bytes 786440 | tf_op jit(solution)/shard_map/ppermute | solution.py:73
  91.6 9.5 %collective-permute-start.12 = (f32[2,2,16,8,128]{4,3,2,1,0:T(8,128)S(1)}, f32[2,2,16,8,128]{4,3,2,1,0:T(8,128)S(1)}, u32[]{:S(2)}, u32[]{:S(2)}) collective-permute-start(f32[2,2,16,8,128]{4,3,2,1,0:T(8,128)S(1)} %get-tuple-element.41), channel_id=1, source_target_pairs={{0,12},{1,13},{2,14},{3,15},{4,0},{5,1},{6,2},{7,3},{8,4},{9,5},{1... | collective-permute-start | bytes 786440 | tf_op jit(solution)/shard_map/ppermute | solution.py:73

commit v3 on v2

--- a/solution.py
+++ b/solution.py
@@ -84,45 +84,74 @@
     return b_low, b_high, c_low, c_high
 
 
-def advance(swap, steps, here, beside, beyond, y_back, y_next, z_back, z_next, open_cells, put):
+def own_part(steps, here, beside, put):
     b_low, b_high, c_low, c_high = ladder_rows()
     depth = lax.broadcasted_iota(jnp.int32, (COLS, LANES), 0)
     at_start = depth == 0
     at_end = depth == COLS - 1
 
     def block(g, carry):
-        far = g if swap is None else jnp.where(swap, 1 - g, g)
         for y in range(ROWS):
-
-            def sides(a):
-                near = beside[g, a, y]
-                other = beyond[far, a, y]
-                return near - other, near + other
-
-            is_open = open_cells[g, y]
-            before = None
-            now = sides(0)
             for a in range(MA):
-                after = sides(a + 1) if a + 1 < MA else None
                 f = here[g, a, y]
-                yb = here[g, a, y - 1] if y > 0 else y_back[g, a]
-                yn = here[g, a, y + 1] if y + 1 < ROWS else y_next[g, a]
-                zb = jnp.where(at_start, z_back[g, a, y : y + 1, :], pltpu.roll(f, 1, 0))
-                zn = jnp.where(at_end, z_next[g, a, y : y + 1, :], pltpu.roll(f, COLS - 1, 0))
-                dy = yn - yb
+                zb = jnp.where(at_start, 0.0, pltpu.roll(f, 1, 0))
+                zn = jnp.where(at_end, 0.0, pltpu.roll(f, COLS - 1, 0))
+                if y == 0:
+                    dy = across = here[g, a, y + 1]
+                elif y == ROWS - 1:
+                    across = here[g, a, y - 1]
+                    dy = -across
+                else:
+                    dy = here[g, a, y + 1] - here[g, a, y - 1]
+                    across = here[g, a, y + 1] + here[g, a, y - 1]
                 dz = zn - zb
-                change = CX * (now[1] + (yn + yb)) + CZ * (zn + zb) - CENTER * f
-                if before is not None:
-                    change = change - steps[a] * before
-                if after is not None:
-                    change = change - steps[a + 1] * after[0]
+                change = CX * (beside[g, a, y] + across) + CZ * (zn + zb) - CENTER * f
+                if a > 0:
+                    change = change - steps[a] * beside[g, a - 1, y]
+                if a + 1 < MA:
+                    change = change - steps[a + 1] * beside[g, a + 1, y]
                 change = change - b_low * pltpu.roll(dy, MC, 1)
                 change = change - b_high * pltpu.roll(dy, LANES - MC, 1)
                 change = change - c_low * pltpu.roll(dz, 1, 1)
                 change = change - c_high * pltpu.roll(dz, LANES - 1, 1)
-                put(g, a, y, f + is_open * change)
-                before = now[0]
-                now = after
+                put(g, a, y, change)
+        return carry
+
+    lax.fori_loop(0, 2, block, 0)
+
+
+def advance(swap, steps, here, change, beyond, y_back, y_next, z_back, z_next, open_cells, ends, put):
+    b_low, b_high, c_low, c_high = ladder_rows()
+    depth = lax.broadcasted_iota(jnp.int32, (COLS, LANES), 0)
+    at_start = depth == 0
+    at_end = depth == COLS - 1
+
+    def ladder(value, low, high, by):
+        return low * pltpu.roll(value, by, 1) + high * pltpu.roll(value, LANES - by, 1)
+
+    def block(g, carry):
+        far = g if swap is None else jnp.where(swap, 1 - g, g)
+        for a in range(MA):
+            back, ahead = z_back[g, a], z_next[g, a]
+            ends[0, a] = CZ * back + ladder(back, c_low, c_high, 1)
+            ends[1, a] = CZ * ahead - ladder(ahead, c_low, c_high, 1)
+        for y in range(ROWS):
+            is_open = open_cells[g, y]
+            for a in range(MA):
+                total = change[g, a, y] + CX * beyond[far, a, y]
+                if a > 0:
+                    total = total + steps[a] * beyond[far, a - 1, y]
+                if a + 1 < MA:
+                    total = total + steps[a + 1] * beyond[far, a + 1, y]
+                if y == 0:
+                    back = y_back[g, a]
+                    total = total + CY * back + ladder(back, b_low, b_high, MC)
+                if y == ROWS - 1:
+                    ahead = y_next[g, a]
+                    total = total + CY * ahead - ladder(ahead, b_low, b_high, MC)
+                last = jnp.where(at_end, ends[1, a, y : y + 1, :], 0.0)
+                total = total + jnp.where(at_start, ends[0, a, y : y + 1, :], last)
+                put(g, a, y, here[g, a, y] + is_open * total)
         return carry
 
     lax.fori_loop(0, 2, block, 0)
@@ -160,28 +189,43 @@
         for which, plane in enumerate(plane_order()):
             cells = jnp.where(source[plane, cols, :] != 0, 0.0, 1.0)
             wide = jnp.concatenate([cells, cells], 1)
-            wide = pltpu.roll(wide, LANES - first_row, 1)
+            wide = pltpu.roll(wide, lax.rem(LANES - first_row, LANES), 1)
             for y in range(ROWS):
                 table[which, g, y] = jnp.broadcast_to(wide[:, y : y + 1], (COLS, LANES))
 
 
-def both_planes(planes, beyond, faces, open_cells, put):
+def ladder_steps(which):
+    sign = jnp.where(lax.axis_index("core") == 0, 1.0, -1.0).astype(jnp.float32)
+    return [(1 - 2 * which) * HALF * math.sqrt(a) * sign for a in range(MA)]
+
+
+def own_kernel(outer_plane, inner_plane, change):
+    planes = (outer_plane, inner_plane)
+    for which in range(2):
+
+        def put(g, a, y, value):
+            change[which, g, a, y] = value
+
+        own_part(ladder_steps(which), planes[which], planes[1 - which], put)
+
+
+def both_planes(planes, change, beyond, faces, open_cells, ends, put):
     column = lax.axis_index("column")
     core = lax.axis_index("core")
-    sign = jnp.where(core == 0, 1.0, -1.0).astype(jnp.float32)
     wraps = ((column == 0) & (core == 0)) | ((column == 3) & (core == 1))
     for which in range(2):
-        steps = [(1 - 2 * which) * HALF * math.sqrt(a) * sign for a in range(MA)]
         advance(
-            wraps if which == 0 else None, steps, planes[which], planes[1 - which], beyond[which],
-            *[face.at[which] for face in faces], open_cells.at[which], functools.partial(put, which),
+            wraps if which == 0 else None, ladder_steps(which), planes[which], change.at[which],
+            beyond[which], *[face.at[which] for face in faces], open_cells.at[which], ends,
+            functools.partial(put, which),
         )
 
 
 def first_kernel(
-    outer_plane, inner_plane, outer_beyond, inner_beyond, y_back, y_next, z_back, z_next,
-    mine, theirs, out_outer, out_inner, open_cells, *edges,
+    outer_plane, inner_plane, change, outer_beyond, inner_beyond, y_back, y_next, z_back, z_next,
+    mine, theirs, out_outer, out_inner, open_cells, out_y0, out_y7, out_z0, out_z7, ends,
 ):
+    edges = (out_y0, out_y7, out_z0, out_z7)
     open_table(mine, theirs, open_cells)
 
     def put(which, g, a, y, value):
@@ -189,8 +233,8 @@
         put_edges(g, a, y, value, *[edge.at[which] for edge in edges])
 
     both_planes(
-        (outer_plane, inner_plane), (outer_beyond, inner_beyond), (y_back, y_next, z_back, z_next),
-        open_cells, put,
+        (outer_plane, inner_plane), change, (outer_beyond, inner_beyond),
+        (y_back, y_next, z_back, z_next), open_cells, ends, put,
     )
 
 
@@ -203,22 +247,27 @@
     return core, 1 - core
 
 
-def gather_blocks(field, blocks, arrived):
-    copies = []
+def gather_blocks(field, blocks, stage, arrived, stored):
+    loads, stores = [], []
     for which, plane in enumerate(plane_order()):
         for half in range(2):
             for row in range(4):
-                copies.append(
+                at = (which, half, row)
+                loads.append(
                     pltpu.make_async_copy(
-                        field.at[plane].at[tile_of(half, row)],
-                        blocks.at[half, row, :, which],
-                        arrived.at[which, half, row],
+                        field.at[plane].at[tile_of(half, row)], stage.at[at], arrived.at[at]
                     )
                 )
-    for copy in copies:
-        copy.start()
-    for copy in copies:
-        copy.wait()
+                stores.append(
+                    pltpu.make_async_copy(stage.at[at], blocks.at[half, row, :, which], stored.at[at])
+                )
+    for load in loads:
+        load.start()
+    for load, store in zip(loads, stores):
+        load.wait()
+        store.start()
+    for store in stores:
+        store.wait()
 
 
 def scatter_blocks(blocks, field, arrived):
@@ -248,15 +297,15 @@
 
 
 def second_kernel(
-    outer_plane, inner_plane, outer_beyond, inner_beyond, y_back, y_next, z_back, z_next,
-    open_cells, selector, weights, out, low, factors,
+    outer_plane, inner_plane, change, outer_beyond, inner_beyond, y_back, y_next, z_back, z_next,
+    open_cells, selector, weights, out, ends, low, factors,
 ):
     def put(which, g, a, y, value):
         out[g, a, which, y] = value
 
     both_planes(
-        (outer_plane, inner_plane), (outer_beyond, inner_beyond), (y_back, y_next, z_back, z_next),
-        open_cells, put,
+        (outer_plane, inner_plane), change, (outer_beyond, inner_beyond),
+        (y_back, y_next, z_back, z_next), open_cells, ends, put,
     )
     cells = 2 * 2 * ROWS * COLS
     lane = lax.broadcasted_iota(jnp.int32, (cells, LANES), 1)
@@ -319,6 +368,7 @@
 
 VMEM = pl.BlockSpec(memory_space=pltpu.VMEM)
 PARAMS = pltpu.CompilerParams(vmem_limit_bytes=16 << 20)
+WHOLE = pltpu.CompilerParams(vmem_limit_bytes=61 << 20)
 HBM = pl.BlockSpec(memory_space=pltpu.HBM)
 COPY_SEMS = [pltpu.SemaphoreType.DMA((2, 2, 4))]
 
@@ -329,6 +379,8 @@
 
 PLANE = f32(2, MA, ROWS, COLS, LANES)
 EDGES = f32(2, 2, MA, ROWS, LANES)
+CHANGE = f32(2, 2, MA, ROWS, COLS, LANES)
+ENDS = pltpu.VMEM((2, MA, ROWS, LANES), jnp.float32)
 
 
 def surroundings(outer_plane, inner_plane, edges):
@@ -343,7 +395,7 @@
     return outer_beyond, inner_beyond, y_back, y_next, z_back, z_next
 
 
-def call(kernel, out_shape, *operands, operand_space=VMEM, out_space=VMEM, scratch=()):
+def call(kernel, out_shape, *operands, operand_space=VMEM, out_space=VMEM, scratch=(), params=PARAMS):
     single = not isinstance(out_shape, tuple)
     return pl.pallas_call(
         kernel,
@@ -351,7 +403,7 @@
         in_specs=[operand_space] * len(operands),
         out_specs=out_space if single else (out_space,) * len(out_shape),
         scratch_shapes=scratch,
-        compiler_params=PARAMS,
+        compiler_params=params,
     )(*operands)
 
 
@@ -364,7 +416,10 @@
     theirs = send(mine, other_half())
     tiles = f32(2, 4, 4, 2, ROWS, COLS, LANES)
     tiled = (2, 2, 4, ROWS, 4 * COLS, LANES)
-    blocks = call(gather_blocks, tiles, field.reshape(tiled), operand_space=HBM, scratch=COPY_SEMS)
+    blocks = call(
+        gather_blocks, tiles, field.reshape(tiled), operand_space=HBM, out_space=HBM, params=WHOLE,
+        scratch=[pltpu.VMEM((2, 2, 4, 4, ROWS, COLS, LANES), jnp.float32)] + COPY_SEMS * 2,
+    )
     state = exchange(blocks.reshape(BLOCKS, 2, ROWS, COLS, LANES))
     state, theirs = lax.optimization_barrier((state, theirs))
 
@@ -372,16 +427,19 @@
         split_kernel, (PLANE,) * 2 + (EDGES,) * 4, state.reshape(2, MA, 2, ROWS, COLS, LANES)
     )
     around = surroundings(outer_plane, inner_plane, edges)
+    change = call(own_kernel, CHANGE, outer_plane, inner_plane)
     outer_plane, inner_plane, open_cells, *edges = call(
         first_kernel, (PLANE,) * 2 + (f32(2, 2, ROWS, COLS, LANES),) + (EDGES,) * 4,
-        outer_plane, inner_plane, *around, mine, theirs,
+        outer_plane, inner_plane, change, *around, mine, theirs, scratch=[ENDS],
     )
     around = surroundings(outer_plane, inner_plane, edges)
+    change = call(own_kernel, CHANGE, outer_plane, inner_plane)
     cells = 2 * 2 * ROWS * COLS
     state = call(
         second_kernel, f32(2, MA, 2, ROWS, COLS, LANES),
-        outer_plane, inner_plane, *around, open_cells, low_selector(), kernel_table.T,
+        outer_plane, inner_plane, change, *around, open_cells, low_selector(), kernel_table.T,
         scratch=[
+            ENDS,
             pltpu.VMEM((PAD, cells), jnp.float32),
             pltpu.VMEM((2, GROUP * BASIS_SIZE, cells), jnp.bfloat16),
         ],

time: 166 us -> 163 us (0.982)
  waiting for transfers between devices: 61.1 us -> 56.2 us
  Pallas kernels: 11.6 us -> 15.8 us
  local copies, waits for them, and re-layouts: 2.92 us -> 0.01 us
    ppermute x13, waiting for transfers between devices: 61.1 us -> 56.2 us  [send(): return lax.ppermute(value, AXES, route)]
    pallas_call x5 -> x7, Pallas kernels: 11.6 us -> 15.8 us  [call(): pl.pallas_call(kernel, out_shape=out_shape, in_specs=[operand_space] * le...]
    unnamed x10 -> x6, local copies, waits for them, and re-layouts: 2.92 us -> 0.01 us
  transfers between devices with their start and end apart: 14 -> 14, of which waited for: 7 -> 7; matrix products, arithmetic and copies ran while one was open for 0% -> 0% of each run, Pallas kernels for 0% -> 3%
where the time goes in v3:
time: 163 us; the launch traced here: 162 us
  blocking collectives  56.9 us (35%)
  waiting for transfers between devices  56.2 us (34%)
  starting transfers between devices  33 us (20%)
  Pallas kernels  15.8 us (10%)
    all_to_all x1, blocking collectives, exchange(): return lax.all_to_all(blocks, ('half', 'row', 'run'), 0, 0, tiled=True)  56.9 us
    ppermute x13, waiting for transfers between devices, send(): return lax.ppermute(value, AXES, route)  56.2 us
    ppermute x13, starting transfers between devices, send(): return lax.ppermute(value, AXES, route)  21.5 us
    pallas_call x7, Pallas kernels, call(): pl.pallas_call(kernel, out_shape=out_shape, in_specs=[operand_space] * le...  15.8 us
    all_to_all x1, starting transfers between devices, exchange(): return lax.all_to_all(blocks, ('half', 'row', 'run'), 0, 0, tiled=True)  11.5 us
  transfers between devices with their start and end apart: 14, of which 7 were waited for; matrix products, arithmetic and copies ran while one was open for 0% of the time, Pallas kernels for 3%

profile of v3, /device:TPU:6, one launch (start us, length us, event | category | flops | bytes accessed | tf_op | source)
XLA Modules:
  0.0 162.1 jit_solution(11416303109068848463)
XLA Ops:
  0.0 2.6 %shard_map.46 = f32[2,4,4,2,8,8,128]{6,5,4,3,2,1,0:T(8,128)} custom-call(f32[2,2,4,8,32,128]{5,4,3,2,1,0:T(8,128)} %bitcast.15), custom_call_target="tpu_custom_call" | custom-call | tf_op jit(solution)/shard_map/pallas_call | solution.py:400
  2.6 0.0 copy-start.2
  2.6 11.5 %all-to-all-start = ((f32[32,2,8,8,128]{4,3,2,1,0:T(8,128)}), f32[32,2,8,8,128]{4,3,2,1,0:T(8,128)S(1)}, u32[]{:S(2)}, u32[]{:S(2)}) async-start(f32[32,2,8,8,128]{4,3,2,1,0:T(8,128)} %bitcast.14), calls=%async_computation | async-start | bytes 4194304 | tf_op jit(solution)/shard_map/all_to_all | solution.py:411
  14.1 5.8 %collective-permute-start = (s32[2,32,64]{2,1,0:T(8,128)S(1)}, s32[2,32,64]{2,1,0:T(8,128)S(1)}, u32[]{:S(2)}, u32[]{:S(2)}) collective-permute-start(s32[2,32,64]{2,1,0:T(8,128)S(1)} %bitcast.12), channel_id=1, source_target_pairs={{0,128},{1,129},{2,130},{3,131},{4,132},{5,133},{6,134},{7,135},{8... | collective-permute-start | bytes 49160 | tf_op jit(solution)/shard_map/ppermute | solution.py:73
  19.9 46.5 %collective-permute-done.theirs = s32[2,32,64]{2,1,0:T(8,128)S(1)} collective-permute-done((s32[2,32,64]{2,1,0:T(8,128)S(1)}, s32[2,32,64]{2,1,0:T(8,128)S(1)}, u32[]{:S(2)}, u32[]{:S(2)}) %collective-permute-start) | collective-permute-done | bytes 16416 | tf_op jit(solution)/shard_map/ppermute | solution.py:73
  66.4 0.7 shard_map.47
  67.1 0.1 collective-permute-start.2
  67.2 0.9 collective-permute-start.1
  68.1 0.6 collective-permute-start.3
  68.7 2.7 %collective-permute-start.4 = (f32[2,2,16,8,128]{4,3,2,1,0:T(8,128)S(1)}, f32[2,2,16,8,128]{4,3,2,1,0:T(8,128)S(1)}, u32[]{:S(2)}, u32[]{:S(2)}) collective-permute-start(f32[2,2,16,8,128]{4,3,2,1,0:T(8,128)S(1)} %get-tuple-element.30), channel_id=1, source_target_pairs={{0,131},{1,0},{2,1},{3,2},{4,135},{5,4},{6,5},{7,6},{8,139},{9,8},... | collective-permute-start | bytes 786440 | tf_op jit(solution)/shard_map/ppermute | solution.py:73
  71.3 1.5 collective-permute-start.5
  72.8 1.8 %collective-permute-start.6 = (f32[2,2,16,8,128]{4,3,2,1,0:T(8,128)S(1)}, f32[2,2,16,8,128]{4,3,2,1,0:T(8,128)S(1)}, u32[]{:S(2)}, u32[]{:S(2)}) collective-permute-start(f32[2,2,16,8,128]{4,3,2,1,0:T(8,128)S(1)} %get-tuple-element.32), channel_id=1, source_target_pairs={{0,12},{1,13},{2,14},{3,15},{4,0},{5,1},{6,2},{7,3},{8,4},{9,5},{1... | collective-permute-start | bytes 786440 | tf_op jit(solution)/shard_map/ppermute | solution.py:73
  74.6 2.4 %shard_map.48.change = f32[2,2,16,8,8,128]{5,4,3,2,1,0:T(8,128)S(1)} custom-call(f32[2,16,8,8,128]{4,3,2,1,0:T(8,128)S(1)} %get-tuple-element.25.outer_plane, f32[2,16,8,8,128]{4,3,2,1,0:T(8,128)S(1)} %get-tuple-element.26.inner_plane), custom_call_target="tpu_custom_call" | custom-call | tf_op jit(solution)/shard_map/pallas_call | solution.py:400
  77.0 0.2 collective-permute-done.3.y_back
  77.3 0.0 collective-permute-done.4.y_next
  77.3 2.7 %collective-permute-done.5.z_back = f32[2,2,16,8,128]{4,3,2,1,0:T(8,128)S(1)} collective-permute-done((f32[2,2,16,8,128]{4,3,2,1,0:T(8,128)S(1)}, f32[2,2,16,8,128]{4,3,2,1,0:T(8,128)S(1)}, u32[]{:S(2)}, u32[]{:S(2)}) %collective-permute-start.5) | collective-permute-done | bytes 262176 | tf_op jit(solution)/shard_map/ppermute | solution.py:73
  80.0 1.5 collective-permute-done.1.outer_beyond
  81.5 1.5 shard_map.49
  82.9 1.7 %collective-permute-start.8 = (f32[2,16,8,8,128]{4,3,2,1,0:T(8,128)S(1)}, f32[2,16,8,8,128]{4,3,2,1,0:T(8,128)S(1)}, u32[]{:S(2)}, u32[]{:S(2)}) collective-permute-start(f32[2,16,8,8,128]{4,3,2,1,0:T(8,128)S(1)} %get-tuple-element.35.inner_plane), channel_id=1, source_target_pairs={{0,16},{1,17},{2,18},{3,19},{4,20},{5,21},{6,22},{7,23},{8,24},{9,... | collective-permute-start | bytes 3145736 | tf_op jit(solution)/shard_map/ppermute | solution.py:73
  84.7 0.6 collective-permute-start.9
  85.2 2.7 %collective-permute-start.10 = (f32[2,2,16,8,128]{4,3,2,1,0:T(8,128)S(1)}, f32[2,2,16,8,128]{4,3,2,1,0:T(8,128)S(1)}, u32[]{:S(2)}, u32[]{:S(2)}) collective-permute-start(f32[2,2,16,8,128]{4,3,2,1,0:T(8,128)S(1)} %get-tuple-element.39), channel_id=1, source_target_pairs={{0,131},{1,0},{2,1},{3,2},{4,135},{5,4},{6,5},{7,6},{8,139},{9,8},... | collective-permute-start | bytes 786440 | tf_op jit(solution)/shard_map/ppermute | solution.py:73
  87.9 1.5 collective-permute-start.11
  89.4 0.0 collective-permute-done.8.inner_beyond
  89.4 1.8 %collective-permute-start.12 = (f32[2,2,16,8,128]{4,3,2,1,0:T(8,128)S(1)}, f32[2,2,16,8,128]{4,3,2,1,0:T(8,128)S(1)}, u32[]{:S(2)}, u32[]{:S(2)}) collective-permute-start(f32[2,2,16,8,128]{4,3,2,1,0:T(8,128)S(1)} %get-tuple-element.41), channel_id=1, source_target_pairs={{0,12},{1,13},{2,14},{3,15},{4,0},{5,1},{6,2},{7,3},{8,4},{9,5},{1... | collective-permute-start | bytes 786440 | tf_op jit(solution)/shard_map/ppermute | solution.py:73
  91.1 2.4 %shard_map.50.change = f32[2,2,16,8,8,128]{5,4,3,2,1,0:T(8,128)S(1)} custom-call(f32[2,16,8,8,128]{4,3,2,1,0:T(8,128)S(1)} %get-tuple-element.34.outer_plane, f32[2,16,8,8,128]{4,3,2,1,0:T(8,128)S(1)} %get-tuple-element.35.inner_plane), custom_call_target="tpu_custom_call" | custom-call | tf_op jit(solution)/shard_map/pallas_call | solution.py:400
  93.6 0.8 collective-permute-done.9.y_back
  94.4 0.0 collective-permute-done.10.y_next
  94.4 2.7 %collective-permute-done.11.z_back = f32[2,2,16,8,128]{4,3,2,1,0:T(8,128)S(1)} collective-permute-done((f32[2,2,16,8,128]{4,3,2,1,0:T(8,128)S(1)}, f32[2,2,16,8,128]{4,3,2,1,0:T(8,128)S(1)}, u32[]{:S(2)}, u32[]{:S(2)}) %collective-permute-start.11) | collective-permute-done | bytes 262176 | tf_op jit(solution)/shard_map/ppermute | solution.py:73
  97.0 1.8 %collective-permute-done.7.outer_beyond = f32[2,16,8,8,128]{4,3,2,1,0:T(8,128)S(1)} collective-permute-done((f32[2,16,8,8,128]{4,3,2,1,0:T(8,128)S(1)}, f32[2,16,8,8,128]{4,3,2,1,0:T(8,128)S(1)}, u32[]{:S(2)}, u32[]{:S(2)}) %collective-permute-start.7) | collective-permute-done | bytes 1048608 | tf_op jit(solution)/shard_map/ppermute | solution.py:73
  98.9 4.7 %shard_map.51 = f32[2,16,2,8,8,128]{5,4,3,2,1,0:T(8,128)S(1)} custom-call(f32[2,16,8,8,128]{4,3,2,1,0:T(8,128)S(1)} %get-tuple-element.34.outer_plane, f32[2,16,8,8,128]{4,3,2,1,0:T(8,128)S(1)} %get-tuple-element.35.inner_plane, f32[2,2,16,8,8,128]{5,4,3,2,1,0:T(8,128)S(1)} %shard_map.50.change, ...), custom_call_target="tpu_custom_call" | custom-call | tf_op jit(solution)/shard_map/pallas_call | solution.py:400
  103.6 56.9 %all_to_all.10 = f32[32,2,8,8,128]{4,3,2,1,0:T(8,128)S(1)} all-to-all(f32[32,2,8,8,128]{4,3,2,1,0:T(8,128)S(1)} %bitcast.10), channel_id=1, replica_groups=mesh['half'=2,'column'=4,'core'=2,'row'=4,'run'=4] {'half','row','run'}, dimensions={0} | all-to-all | bytes 4194304 | tf_op jit(solution)/shard_map/all_to_all | solution.py:411
  160.5 1.4 shard_map.52
  (10 shorter events, 0.0 us)
Async XLA Ops:
  2.6 11.5 %copy-start.2 = (s32[2,64,32]{1,2,0:T(8,128)S(1)}, s32[2,64,32]{1,2,0:T(8,128)}, u32[]{:S(2)}) copy-start(s32[2,64,32]{1,2,0:T(8,128)} %param.6) | copy-start | bytes 49156
  2.6 63.8 %all-to-all-start = ((f32[32,2,8,8,128]{4,3,2,1,0:T(8,128)}), f32[32,2,8,8,128]{4,3,2,1,0:T(8,128)S(1)}, u32[]{:S(2)}, u32[]{:S(2)}) async-start(f32[32,2,8,8,128]{4,3,2,1,0:T(8,128)} %bitcast.14), calls=%async_computation | async-start | bytes 4194304 | tf_op jit(solution)/shard_map/all_to_all | solution.py:411
  14.1 52.3 %collective-permute-start = (s32[2,32,64]{2,1,0:T(8,128)S(1)}, s32[2,32,64]{2,1,0:T(8,128)S(1)}, u32[]{:S(2)}, u32[]{:S(2)}) collective-permute-start(s32[2,32,64]{2,1,0:T(8,128)S(1)} %bitcast.12), channel_id=1, source_target_pairs={{0,128},{1,129},{2,130},{3,131},{4,132},{5,133},{6,134},{7,135},{8... | collective-permute-start | bytes 49160 | tf_op jit(solution)/shard_map/ppermute | solution.py:73
  67.1 5.7 %collective-permute-start.2 = (f32[2,16,8,8,128]{4,3,2,1,0:T(8,128)S(1)}, f32[2,16,8,8,128]{4,3,2,1,0:T(8,128)S(1)}, u32[]{:S(2)}, u32[]{:S(2)}) collective-permute-start(f32[2,16,8,8,128]{4,3,2,1,0:T(8,128)S(1)} %get-tuple-element.26.inner_plane), channel_id=1, source_target_pairs={{0,16},{1,17},{2,18},{3,19},{4,20},{5,21},{6,22},{7,23},{8,24},{9,... | collective-permute-start | bytes 3145736 | tf_op jit(solution)/shard_map/ppermute | solution.py:73
  67.2 14.3 %collective-permute-start.1 = (f32[2,16,8,8,128]{4,3,2,1,0:T(8,128)S(1)}, f32[2,16,8,8,128]{4,3,2,1,0:T(8,128)S(1)}, u32[]{:S(2)}, u32[]{:S(2)}) collective-permute-start(f32[2,16,8,8,128]{4,3,2,1,0:T(8,128)S(1)} %get-tuple-element.25.outer_plane), channel_id=1, source_target_pairs={{0,112},{1,113},{2,114},{3,115},{4,116},{5,117},{6,118},{7,119},{8... | collective-permute-start | bytes 3145736 | tf_op jit(solution)/shard_map/ppermute | solution.py:73
  68.1 9.2 %collective-permute-start.3 = (f32[2,2,16,8,128]{4,3,2,1,0:T(8,128)S(1)}, f32[2,2,16,8,128]{4,3,2,1,0:T(8,128)S(1)}, u32[]{:S(2)}, u32[]{:S(2)}) collective-permute-start(f32[2,2,16,8,128]{4,3,2,1,0:T(8,128)S(1)} %get-tuple-element.29), channel_id=1, source_target_pairs={{0,1},{1,2},{2,3},{3,128},{4,5},{5,6},{6,7},{7,132},{8,9},{9,10},{... | collective-permute-start | bytes 786440 | tf_op jit(solution)/shard_map/ppermute | solution.py:73
  68.7 8.6 %collective-permute-start.4 = (f32[2,2,16,8,128]{4,3,2,1,0:T(8,128)S(1)}, f32[2,2,16,8,128]{4,3,2,1,0:T(8,128)S(1)}, u32[]{:S(2)}, u32[]{:S(2)}) collective-permute-start(f32[2,2,16,8,128]{4,3,2,1,0:T(8,128)S(1)} %get-tuple-element.30), channel_id=1, source_target_pairs={{0,131},{1,0},{2,1},{3,2},{4,135},{5,4},{6,5},{7,6},{8,139},{9,8},... | collective-permute-start | bytes 786440 | tf_op jit(solution)/shard_map/ppermute | solution.py:73
  71.3 8.6 %collective-permute-start.5 = (f32[2,2,16,8,128]{4,3,2,1,0:T(8,128)S(1)}, f32[2,2,16,8,128]{4,3,2,1,0:T(8,128)S(1)}, u32[]{:S(2)}, u32[]{:S(2)}) collective-permute-start(f32[2,2,16,8,128]{4,3,2,1,0:T(8,128)S(1)} %get-tuple-element.31), channel_id=1, source_target_pairs={{0,4},{1,5},{2,6},{3,7},{4,8},{5,9},{6,10},{7,11},{8,12},{9,13},{1... | collective-permute-start | bytes 786440 | tf_op jit(solution)/shard_map/ppermute | solution.py:73
  72.8 8.7 %collective-permute-start.6 = (f32[2,2,16,8,128]{4,3,2,1,0:T(8,128)S(1)}, f32[2,2,16,8,128]{4,3,2,1,0:T(8,128)S(1)}, u32[]{:S(2)}, u32[]{:S(2)}) collective-permute-start(f32[2,2,16,8,128]{4,3,2,1,0:T(8,128)S(1)} %get-tuple-element.32), channel_id=1, source_target_pairs={{0,12},{1,13},{2,14},{3,15},{4,0},{5,1},{6,2},{7,3},{8,4},{9,5},{1... | collective-permute-start | bytes 786440 | tf_op jit(solution)/shard_map/ppermute | solution.py:73
  82.9 6.4 %collective-permute-start.8 = (f32[2,16,8,8,128]{4,3,2,1,0:T(8,128)S(1)}, f32[2,16,8,8,128]{4,3,2,1,0:T(8,128)S(1)}, u32[]{:S(2)}, u32[]{:S(2)}) collective-permute-start(f32[2,16,8,8,128]{4,3,2,1,0:T(8,128)S(1)} %get-tuple-element.35.inner_plane), channel_id=1, source_target_pairs={{0,16},{1,17},{2,18},{3,19},{4,20},{5,21},{6,22},{7,23},{8,24},{9,... | collective-permute-start | bytes 3145736 | tf_op jit(solution)/shard_map/ppermute | solution.py:73
  84.7 14.2 %collective-permute-start.7 = (f32[2,16,8,8,128]{4,3,2,1,0:T(8,128)S(1)}, f32[2,16,8,8,128]{4,3,2,1,0:T(8,128)S(1)}, u32[]{:S(2)}, u32[]{:S(2)}) collective-permute-start(f32[2,16,8,8,128]{4,3,2,1,0:T(8,128)S(1)} %get-tuple-element.34.outer_plane), channel_id=1, source_target_pairs={{0,112},{1,113},{2,114},{3,115},{4,116},{5,117},{6,118},{7,119},{8... | collective-permute-start | bytes 3145736 | tf_op jit(solution)/shard_map/ppermute | solution.py:73
  84.7 9.7 %collective-permute-start.9 = (f32[2,2,16,8,128]{4,3,2,1,0:T(8,128)S(1)}, f32[2,2,16,8,128]{4,3,2,1,0:T(8,128)S(1)}, u32[]{:S(2)}, u32[]{:S(2)}) collective-permute-start(f32[2,2,16,8,128]{4,3,2,1,0:T(8,128)S(1)} %get-tuple-element.38), channel_id=1, source_target_pairs={{0,1},{1,2},{2,3},{3,128},{4,5},{5,6},{6,7},{7,132},{8,9},{9,10},{... | collective-permute-start | bytes 786440 | tf_op jit(solution)/shard_map/ppermute | solution.py:73
  85.2 9.1 %collective-permute-start.10 = (f32[2,2,16,8,128]{4,3,2,1,0:T(8,128)S(1)}, f32[2,2,16,8,128]{4,3,2,1,0:T(8,128)S(1)}, u32[]{:S(2)}, u32[]{:S(2)}) collective-permute-start(f32[2,2,16,8,128]{4,3,2,1,0:T(8,128)S(1)} %get-tuple-element.39), channel_id=1, source_target_pairs={{0,131},{1,0},{2,1},{3,2},{4,135},{5,4},{6,5},{7,6},{8,139},{9,8},... | collective-permute-start | bytes 786440 | tf_op jit(solution)/shard_map/ppermute | solution.py:73
  87.9 9.1 %collective-permute-start.11 = (f32[2,2,16,8,128]{4,3,2,1,0:T(8,128)S(1)}, f32[2,2,16,8,128]{4,3,2,1,0:T(8,128)S(1)}, u32[]{:S(2)}, u32[]{:S(2)}) collective-permute-start(f32[2,2,16,8,128]{4,3,2,1,0:T(8,128)S(1)} %get-tuple-element.40), channel_id=1, source_target_pairs={{0,4},{1,5},{2,6},{3,7},{4,8},{5,9},{6,10},{7,11},{8,12},{9,13},{1... | collective-permute-start | bytes 786440 | tf_op jit(solution)/shard_map/ppermute | solution.py:73
  89.4 9.5 %copy-start = (bf16[14400,120]{0,1:T(8,128)(2,1)S(1)}, bf16[14400,120]{0,1:T(8,128)(2,1)}, u32[]{:S(2)}) copy-start(bf16[14400,120]{0,1:T(8,128)(2,1)} %param.5) | copy-start | bytes 10368004
  89.4 9.5 %copy-start.1 = (bf16[4,128,128]{2,1,0:T(8,128)(2,1)S(1)}, bf16[4,128,128]{2,1,0:T(8,128)(2,1)}, u32[]{:S(2)}) copy-start(bf16[4,128,128]{2,1,0:T(8,128)(2,1)} %constant.2.clone.selector) | copy-start | bytes 393220
  89.4 9.5 %collective-permute-start.12 = (f32[2,2,16,8,128]{4,3,2,1,0:T(8,128)S(1)}, f32[2,2,16,8,128]{4,3,2,1,0:T(8,128)S(1)}, u32[]{:S(2)}, u32[]{:S(2)}) collective-permute-start(f32[2,2,16,8,128]{4,3,2,1,0:T(8,128)S(1)} %get-tuple-element.41), channel_id=1, source_target_pairs={{0,12},{1,13},{2,14},{3,15},{4,0},{5,1},{6,2},{7,3},{8,4},{9,5},{1... | collective-permute-start | bytes 786440 | tf_op jit(solution)/shard_map/ppermute | solution.py:73

commit v4 on v3

--- a/solution.py
+++ b/solution.py
@@ -137,12 +137,15 @@
             ends[1, a] = CZ * ahead - ladder(ahead, c_low, c_high, 1)
         for y in range(ROWS):
             is_open = open_cells[g, y]
+            before, now = None, beyond[far, 0, y]
             for a in range(MA):
-                total = change[g, a, y] + CX * beyond[far, a, y]
-                if a > 0:
-                    total = total + steps[a] * beyond[far, a - 1, y]
-                if a + 1 < MA:
-                    total = total + steps[a + 1] * beyond[far, a + 1, y]
+                after = beyond[far, a + 1, y] if a + 1 < MA else None
+                total = change[g, a, y] + CX * now
+                if before is not None:
+                    total = total + steps[a] * before
+                if after is not None:
+                    total = total + steps[a + 1] * after
+                before, now = now, after
                 if y == 0:
                     back = y_back[g, a]
                     total = total + CY * back + ladder(back, b_low, b_high, MC)
@@ -166,7 +169,7 @@
     out_z7[g, a, y : y + 1, :] = value[COLS - 1 : COLS]
 
 
-def split_kernel(state, out_outer, out_inner, *edges):
+def split_kernel(state, out_outer, out_inner, out_y0, out_y7, out_z0, out_z7):
     def block(index, carry):
         g = index // MA
         a = index % MA
@@ -174,10 +177,15 @@
             for y in range(ROWS):
                 value = state[g, a, which, y]
                 out[g, a, y] = value
-                put_edges(g, a, y, value, *[edge.at[which] for edge in edges])
+                if y == 0:
+                    out_y0[which, g, a] = value
+                if y == ROWS - 1:
+                    out_y7[which, g, a] = value
+            out_z0[which, g, a] = state[g, a, which, :, 0, :]
+            out_z7[which, g, a] = state[g, a, which, :, COLS - 1, :]
         return carry
 
-    lax.fori_loop(0, 2 * MA, block, 0)
+    lax.fori_loop(0, 2 * MA, block, 0, unroll=4)
 
 
 def open_table(mine, theirs, table):
@@ -337,7 +345,7 @@
             preferred_element_type=jnp.float32,
         )
     rate = jnp.concatenate([rate, jnp.zeros((PAD - BASIS_SIZE, cells), jnp.float32)], 0)
-    rate_parts = three_parts(jnp.transpose(DTC * rate))
+    rate_parts = three_parts(jnp.transpose(DTC * rate))[:2]
     for a in range(0, LOW_A, 2):
         lifted = jnp.zeros((cells, LANES), jnp.float32)
         for part in rate_parts:

time: 163 us -> 162 us (level)
  no operation moved by 1% of the time
where the time goes in v4:
time: 162 us
  blocking collectives  56.9 us (35%)
  waiting for transfers between devices  56.2 us (35%)
  starting transfers between devices  33 us (20%)
  Pallas kernels  15.4 us (10%)
    all_to_all x1, blocking collectives, exchange(): return lax.all_to_all(blocks, ('half', 'row', 'run'), 0, 0, tiled=True)  56.9 us
    ppermute x13, waiting for transfers between devices, send(): return lax.ppermute(value, AXES, route)  56.2 us
    ppermute x13, starting transfers between devices, send(): return lax.ppermute(value, AXES, route)  21.5 us
    pallas_call x7, Pallas kernels, call(): pl.pallas_call(kernel, out_shape=out_shape, in_specs=[operand_space] * le...  15.4 us
    all_to_all x1, starting transfers between devices, exchange(): return lax.all_to_all(blocks, ('half', 'row', 'run'), 0, 0, tiled=True)  11.5 us
  transfers between devices with their start and end apart: 14, of which 7 were waited for; matrix products, arithmetic and copies ran while one was open for 0% of the time, Pallas kernels for 3%

profile of v4, /device:TPU:6, one launch (start us, length us, event | category | flops | bytes accessed | tf_op | source)
XLA Modules:
  0.0 161.8 jit_solution(525704610720836934)
XLA Ops:
  0.0 2.6 %shard_map.46 = f32[2,4,4,2,8,8,128]{6,5,4,3,2,1,0:T(8,128)} custom-call(f32[2,2,4,8,32,128]{5,4,3,2,1,0:T(8,128)} %bitcast.15), custom_call_target="tpu_custom_call" | custom-call | tf_op jit(solution)/shard_map/pallas_call | solution.py:408
  2.6 0.0 copy-start.2
  2.6 11.5 %all-to-all-start = ((f32[32,2,8,8,128]{4,3,2,1,0:T(8,128)}), f32[32,2,8,8,128]{4,3,2,1,0:T(8,128)S(1)}, u32[]{:S(2)}, u32[]{:S(2)}) async-start(f32[32,2,8,8,128]{4,3,2,1,0:T(8,128)} %bitcast.14), calls=%async_computation | async-start | bytes 4194304 | tf_op jit(solution)/shard_map/all_to_all | solution.py:419
  14.1 5.8 %collective-permute-start = (s32[2,32,64]{2,1,0:T(8,128)S(1)}, s32[2,32,64]{2,1,0:T(8,128)S(1)}, u32[]{:S(2)}, u32[]{:S(2)}) collective-permute-start(s32[2,32,64]{2,1,0:T(8,128)S(1)} %bitcast.12), channel_id=1, source_target_pairs={{0,128},{1,129},{2,130},{3,131},{4,132},{5,133},{6,134},{7,135},{8... | collective-permute-start | bytes 49160 | tf_op jit(solution)/shard_map/ppermute | solution.py:73
  19.9 46.5 %collective-permute-done.theirs = s32[2,32,64]{2,1,0:T(8,128)S(1)} collective-permute-done((s32[2,32,64]{2,1,0:T(8,128)S(1)}, s32[2,32,64]{2,1,0:T(8,128)S(1)}, u32[]{:S(2)}, u32[]{:S(2)}) %collective-permute-start) | collective-permute-done | bytes 16416 | tf_op jit(solution)/shard_map/ppermute | solution.py:73
  66.4 0.5 shard_map.47
  66.9 0.1 collective-permute-start.2
  67.0 0.9 collective-permute-start.1
  67.9 0.6 collective-permute-start.3
  68.5 2.7 %collective-permute-start.4 = (f32[2,2,16,8,128]{4,3,2,1,0:T(8,128)S(1)}, f32[2,2,16,8,128]{4,3,2,1,0:T(8,128)S(1)}, u32[]{:S(2)}, u32[]{:S(2)}) collective-permute-start(f32[2,2,16,8,128]{4,3,2,1,0:T(8,128)S(1)} %get-tuple-element.30), channel_id=1, source_target_pairs={{0,131},{1,0},{2,1},{3,2},{4,135},{5,4},{6,5},{7,6},{8,139},{9,8},... | collective-permute-start | bytes 786440 | tf_op jit(solution)/shard_map/ppermute | solution.py:73
  71.1 1.5 collective-permute-start.5
  72.6 1.8 %collective-permute-start.6 = (f32[2,2,16,8,128]{4,3,2,1,0:T(8,128)S(1)}, f32[2,2,16,8,128]{4,3,2,1,0:T(8,128)S(1)}, u32[]{:S(2)}, u32[]{:S(2)}) collective-permute-start(f32[2,2,16,8,128]{4,3,2,1,0:T(8,128)S(1)} %get-tuple-element.32), channel_id=1, source_target_pairs={{0,12},{1,13},{2,14},{3,15},{4,0},{5,1},{6,2},{7,3},{8,4},{9,5},{1... | collective-permute-start | bytes 786440 | tf_op jit(solution)/shard_map/ppermute | solution.py:73
  74.4 2.4 %shard_map.48.change = f32[2,2,16,8,8,128]{5,4,3,2,1,0:T(8,128)S(1)} custom-call(f32[2,16,8,8,128]{4,3,2,1,0:T(8,128)S(1)} %get-tuple-element.25.outer_plane, f32[2,16,8,8,128]{4,3,2,1,0:T(8,128)S(1)} %get-tuple-element.26.inner_plane), custom_call_target="tpu_custom_call" | custom-call | tf_op jit(solution)/shard_map/pallas_call | solution.py:408
  76.8 0.2 collective-permute-done.3.y_back
  77.1 0.0 collective-permute-done.4.y_next
  77.1 2.7 %collective-permute-done.5.z_back = f32[2,2,16,8,128]{4,3,2,1,0:T(8,128)S(1)} collective-permute-done((f32[2,2,16,8,128]{4,3,2,1,0:T(8,128)S(1)}, f32[2,2,16,8,128]{4,3,2,1,0:T(8,128)S(1)}, u32[]{:S(2)}, u32[]{:S(2)}) %collective-permute-start.5) | collective-permute-done | bytes 262176 | tf_op jit(solution)/shard_map/ppermute | solution.py:73
  79.8 1.5 collective-permute-done.1.outer_beyond
  81.3 1.5 shard_map.49
  82.7 1.7 %collective-permute-start.8 = (f32[2,16,8,8,128]{4,3,2,1,0:T(8,128)S(1)}, f32[2,16,8,8,128]{4,3,2,1,0:T(8,128)S(1)}, u32[]{:S(2)}, u32[]{:S(2)}) collective-permute-start(f32[2,16,8,8,128]{4,3,2,1,0:T(8,128)S(1)} %get-tuple-element.35.inner_plane), channel_id=1, source_target_pairs={{0,16},{1,17},{2,18},{3,19},{4,20},{5,21},{6,22},{7,23},{8,24},{9,... | collective-permute-start | bytes 3145736 | tf_op jit(solution)/shard_map/ppermute | solution.py:73
  84.5 0.6 collective-permute-start.9
  85.0 2.7 %collective-permute-start.10 = (f32[2,2,16,8,128]{4,3,2,1,0:T(8,128)S(1)}, f32[2,2,16,8,128]{4,3,2,1,0:T(8,128)S(1)}, u32[]{:S(2)}, u32[]{:S(2)}) collective-permute-start(f32[2,2,16,8,128]{4,3,2,1,0:T(8,128)S(1)} %get-tuple-element.39), channel_id=1, source_target_pairs={{0,131},{1,0},{2,1},{3,2},{4,135},{5,4},{6,5},{7,6},{8,139},{9,8},... | collective-permute-start | bytes 786440 | tf_op jit(solution)/shard_map/ppermute | solution.py:73
  87.7 1.5 collective-permute-start.11
  89.2 0.0 collective-permute-done.8.inner_beyond
  89.2 1.8 %collective-permute-start.12 = (f32[2,2,16,8,128]{4,3,2,1,0:T(8,128)S(1)}, f32[2,2,16,8,128]{4,3,2,1,0:T(8,128)S(1)}, u32[]{:S(2)}, u32[]{:S(2)}) collective-permute-start(f32[2,2,16,8,128]{4,3,2,1,0:T(8,128)S(1)} %get-tuple-element.41), channel_id=1, source_target_pairs={{0,12},{1,13},{2,14},{3,15},{4,0},{5,1},{6,2},{7,3},{8,4},{9,5},{1... | collective-permute-start | bytes 786440 | tf_op jit(solution)/shard_map/ppermute | solution.py:73
  90.9 2.4 %shard_map.50.change = f32[2,2,16,8,8,128]{5,4,3,2,1,0:T(8,128)S(1)} custom-call(f32[2,16,8,8,128]{4,3,2,1,0:T(8,128)S(1)} %get-tuple-element.34.outer_plane, f32[2,16,8,8,128]{4,3,2,1,0:T(8,128)S(1)} %get-tuple-element.35.inner_plane), custom_call_target="tpu_custom_call" | custom-call | tf_op jit(solution)/shard_map/pallas_call | solution.py:408
  93.4 0.8 collective-permute-done.9.y_back
  94.2 0.0 collective-permute-done.10.y_next
  94.2 2.7 %collective-permute-done.11.z_back = f32[2,2,16,8,128]{4,3,2,1,0:T(8,128)S(1)} collective-permute-done((f32[2,2,16,8,128]{4,3,2,1,0:T(8,128)S(1)}, f32[2,2,16,8,128]{4,3,2,1,0:T(8,128)S(1)}, u32[]{:S(2)}, u32[]{:S(2)}) %collective-permute-start.11) | collective-permute-done | bytes 262176 | tf_op jit(solution)/shard_map/ppermute | solution.py:73
  96.8 1.8 %collective-permute-done.7.outer_beyond = f32[2,16,8,8,128]{4,3,2,1,0:T(8,128)S(1)} collective-permute-done((f32[2,16,8,8,128]{4,3,2,1,0:T(8,128)S(1)}, f32[2,16,8,8,128]{4,3,2,1,0:T(8,128)S(1)}, u32[]{:S(2)}, u32[]{:S(2)}) %collective-permute-start.7) | collective-permute-done | bytes 1048608 | tf_op jit(solution)/shard_map/ppermute | solution.py:73
  98.7 4.6 %shard_map.51 = f32[2,16,2,8,8,128]{5,4,3,2,1,0:T(8,128)S(1)} custom-call(f32[2,16,8,8,128]{4,3,2,1,0:T(8,128)S(1)} %get-tuple-element.34.outer_plane, f32[2,16,8,8,128]{4,3,2,1,0:T(8,128)S(1)} %get-tuple-element.35.inner_plane, f32[2,2,16,8,8,128]{5,4,3,2,1,0:T(8,128)S(1)} %shard_map.50.change, ...), custom_call_target="tpu_custom_call" | custom-call | tf_op jit(solution)/shard_map/pallas_call | solution.py:408
  103.3 56.9 %all_to_all.10 = f32[32,2,8,8,128]{4,3,2,1,0:T(8,128)S(1)} all-to-all(f32[32,2,8,8,128]{4,3,2,1,0:T(8,128)S(1)} %bitcast.10), channel_id=1, replica_groups=mesh['half'=2,'column'=4,'core'=2,'row'=4,'run'=4] {'half','row','run'}, dimensions={0} | all-to-all | bytes 4194304 | tf_op jit(solution)/shard_map/all_to_all | solution.py:419
  160.2 1.4 shard_map.52
  (10 shorter events, 0.0 us)
Async XLA Ops:
  2.6 11.5 %copy-start.2 = (s32[2,64,32]{1,2,0:T(8,128)S(1)}, s32[2,64,32]{1,2,0:T(8,128)}, u32[]{:S(2)}) copy-start(s32[2,64,32]{1,2,0:T(8,128)} %param.6) | copy-start | bytes 49156
  2.6 63.8 %all-to-all-start = ((f32[32,2,8,8,128]{4,3,2,1,0:T(8,128)}), f32[32,2,8,8,128]{4,3,2,1,0:T(8,128)S(1)}, u32[]{:S(2)}, u32[]{:S(2)}) async-start(f32[32,2,8,8,128]{4,3,2,1,0:T(8,128)} %bitcast.14), calls=%async_computation | async-start | bytes 4194304 | tf_op jit(solution)/shard_map/all_to_all | solution.py:419
  14.1 52.3 %collective-permute-start = (s32[2,32,64]{2,1,0:T(8,128)S(1)}, s32[2,32,64]{2,1,0:T(8,128)S(1)}, u32[]{:S(2)}, u32[]{:S(2)}) collective-permute-start(s32[2,32,64]{2,1,0:T(8,128)S(1)} %bitcast.12), channel_id=1, source_target_pairs={{0,128},{1,129},{2,130},{3,131},{4,132},{5,133},{6,134},{7,135},{8... | collective-permute-start | bytes 49160 | tf_op jit(solution)/shard_map/ppermute | solution.py:73
  66.9 5.7 %collective-permute-start.2 = (f32[2,16,8,8,128]{4,3,2,1,0:T(8,128)S(1)}, f32[2,16,8,8,128]{4,3,2,1,0:T(8,128)S(1)}, u32[]{:S(2)}, u32[]{:S(2)}) collective-permute-start(f32[2,16,8,8,128]{4,3,2,1,0:T(8,128)S(1)} %get-tuple-element.26.inner_plane), channel_id=1, source_target_pairs={{0,16},{1,17},{2,18},{3,19},{4,20},{5,21},{6,22},{7,23},{8,24},{9,... | collective-permute-start | bytes 3145736 | tf_op jit(solution)/shard_map/ppermute | solution.py:73
  67.0 14.3 %collective-permute-start.1 = (f32[2,16,8,8,128]{4,3,2,1,0:T(8,128)S(1)}, f32[2,16,8,8,128]{4,3,2,1,0:T(8,128)S(1)}, u32[]{:S(2)}, u32[]{:S(2)}) collective-permute-start(f32[2,16,8,8,128]{4,3,2,1,0:T(8,128)S(1)} %get-tuple-element.25.outer_plane), channel_id=1, source_target_pairs={{0,112},{1,113},{2,114},{3,115},{4,116},{5,117},{6,118},{7,119},{8... | collective-permute-start | bytes 3145736 | tf_op jit(solution)/shard_map/ppermute | solution.py:73
  67.9 9.2 %collective-permute-start.3 = (f32[2,2,16,8,128]{4,3,2,1,0:T(8,128)S(1)}, f32[2,2,16,8,128]{4,3,2,1,0:T(8,128)S(1)}, u32[]{:S(2)}, u32[]{:S(2)}) collective-permute-start(f32[2,2,16,8,128]{4,3,2,1,0:T(8,128)S(1)} %get-tuple-element.29), channel_id=1, source_target_pairs={{0,1},{1,2},{2,3},{3,128},{4,5},{5,6},{6,7},{7,132},{8,9},{9,10},{... | collective-permute-start | bytes 786440 | tf_op jit(solution)/shard_map/ppermute | solution.py:73
  68.5 8.6 %collective-permute-start.4 = (f32[2,2,16,8,128]{4,3,2,1,0:T(8,128)S(1)}, f32[2,2,16,8,128]{4,3,2,1,0:T(8,128)S(1)}, u32[]{:S(2)}, u32[]{:S(2)}) collective-permute-start(f32[2,2,16,8,128]{4,3,2,1,0:T(8,128)S(1)} %get-tuple-element.30), channel_id=1, source_target_pairs={{0,131},{1,0},{2,1},{3,2},{4,135},{5,4},{6,5},{7,6},{8,139},{9,8},... | collective-permute-start | bytes 786440 | tf_op jit(solution)/shard_map/ppermute | solution.py:73
  71.1 8.6 %collective-permute-start.5 = (f32[2,2,16,8,128]{4,3,2,1,0:T(8,128)S(1)}, f32[2,2,16,8,128]{4,3,2,1,0:T(8,128)S(1)}, u32[]{:S(2)}, u32[]{:S(2)}) collective-permute-start(f32[2,2,16,8,128]{4,3,2,1,0:T(8,128)S(1)} %get-tuple-element.31), channel_id=1, source_target_pairs={{0,4},{1,5},{2,6},{3,7},{4,8},{5,9},{6,10},{7,11},{8,12},{9,13},{1... | collective-permute-start | bytes 786440 | tf_op jit(solution)/shard_map/ppermute | solution.py:73
  72.6 8.7 %collective-permute-start.6 = (f32[2,2,16,8,128]{4,3,2,1,0:T(8,128)S(1)}, f32[2,2,16,8,128]{4,3,2,1,0:T(8,128)S(1)}, u32[]{:S(2)}, u32[]{:S(2)}) collective-permute-start(f32[2,2,16,8,128]{4,3,2,1,0:T(8,128)S(1)} %get-tuple-element.32), channel_id=1, source_target_pairs={{0,12},{1,13},{2,14},{3,15},{4,0},{5,1},{6,2},{7,3},{8,4},{9,5},{1... | collective-permute-start | bytes 786440 | tf_op jit(solution)/shard_map/ppermute | solution.py:73
  82.7 6.4 %collective-permute-start.8 = (f32[2,16,8,8,128]{4,3,2,1,0:T(8,128)S(1)}, f32[2,16,8,8,128]{4,3,2,1,0:T(8,128)S(1)}, u32[]{:S(2)}, u32[]{:S(2)}) collective-permute-start(f32[2,16,8,8,128]{4,3,2,1,0:T(8,128)S(1)} %get-tuple-element.35.inner_plane), channel_id=1, source_target_pairs={{0,16},{1,17},{2,18},{3,19},{4,20},{5,21},{6,22},{7,23},{8,24},{9,... | collective-permute-start | bytes 3145736 | tf_op jit(solution)/shard_map/ppermute | solution.py:73
  84.5 14.2 %collective-permute-start.7 = (f32[2,16,8,8,128]{4,3,2,1,0:T(8,128)S(1)}, f32[2,16,8,8,128]{4,3,2,1,0:T(8,128)S(1)}, u32[]{:S(2)}, u32[]{:S(2)}) collective-permute-start(f32[2,16,8,8,128]{4,3,2,1,0:T(8,128)S(1)} %get-tuple-element.34.outer_plane), channel_id=1, source_target_pairs={{0,112},{1,113},{2,114},{3,115},{4,116},{5,117},{6,118},{7,119},{8... | collective-permute-start | bytes 3145736 | tf_op jit(solution)/shard_map/ppermute | solution.py:73
  84.5 9.7 %collective-permute-start.9 = (f32[2,2,16,8,128]{4,3,2,1,0:T(8,128)S(1)}, f32[2,2,16,8,128]{4,3,2,1,0:T(8,128)S(1)}, u32[]{:S(2)}, u32[]{:S(2)}) collective-permute-start(f32[2,2,16,8,128]{4,3,2,1,0:T(8,128)S(1)} %get-tuple-element.38), channel_id=1, source_target_pairs={{0,1},{1,2},{2,3},{3,128},{4,5},{5,6},{6,7},{7,132},{8,9},{9,10},{... | collective-permute-start | bytes 786440 | tf_op jit(solution)/shard_map/ppermute | solution.py:73
  85.0 9.1 %collective-permute-start.10 = (f32[2,2,16,8,128]{4,3,2,1,0:T(8,128)S(1)}, f32[2,2,16,8,128]{4,3,2,1,0:T(8,128)S(1)}, u32[]{:S(2)}, u32[]{:S(2)}) collective-permute-start(f32[2,2,16,8,128]{4,3,2,1,0:T(8,128)S(1)} %get-tuple-element.39), channel_id=1, source_target_pairs={{0,131},{1,0},{2,1},{3,2},{4,135},{5,4},{6,5},{7,6},{8,139},{9,8},... | collective-permute-start | bytes 786440 | tf_op jit(solution)/shard_map/ppermute | solution.py:73
  87.7 9.1 %collective-permute-start.11 = (f32[2,2,16,8,128]{4,3,2,1,0:T(8,128)S(1)}, f32[2,2,16,8,128]{4,3,2,1,0:T(8,128)S(1)}, u32[]{:S(2)}, u32[]{:S(2)}) collective-permute-start(f32[2,2,16,8,128]{4,3,2,1,0:T(8,128)S(1)} %get-tuple-element.40), channel_id=1, source_target_pairs={{0,4},{1,5},{2,6},{3,7},{4,8},{5,9},{6,10},{7,11},{8,12},{9,13},{1... | collective-permute-start | bytes 786440 | tf_op jit(solution)/shard_map/ppermute | solution.py:73
  89.2 9.5 %copy-start = (bf16[14400,120]{0,1:T(8,128)(2,1)S(1)}, bf16[14400,120]{0,1:T(8,128)(2,1)}, u32[]{:S(2)}) copy-start(bf16[14400,120]{0,1:T(8,128)(2,1)} %param.5) | copy-start | bytes 10368004
  89.2 9.5 %copy-start.1 = (bf16[4,128,128]{2,1,0:T(8,128)(2,1)S(1)}, bf16[4,128,128]{2,1,0:T(8,128)(2,1)}, u32[]{:S(2)}) copy-start(bf16[4,128,128]{2,1,0:T(8,128)(2,1)} %constant.2.clone.selector) | copy-start | bytes 393220
  89.2 9.5 %collective-permute-start.12 = (f32[2,2,16,8,128]{4,3,2,1,0:T(8,128)S(1)}, f32[2,2,16,8,128]{4,3,2,1,0:T(8,128)S(1)}, u32[]{:S(2)}, u32[]{:S(2)}) collective-permute-start(f32[2,2,16,8,128]{4,3,2,1,0:T(8,128)S(1)} %get-tuple-element.41), channel_id=1, source_target_pairs={{0,12},{1,13},{2,14},{3,15},{4,0},{5,1},{6,2},{7,3},{8,4},{9,5},{1... | collective-permute-start | bytes 786440 | tf_op jit(solution)/shard_map/ppermute | solution.py:73
